TPU v7x, 256 devices: a whole 4x4x8 slice. The times are simulated.
256 devices in a mesh: seq: 64 (over z, x, core), head: 4 (over y).
Axes of the slice: x: 4, y: 4, z: 8, core: 2. Of those that a mesh axis runs over, the one named last changes fastest.
Arguments:
- queries: float32 [16384, 4096], P('seq', 'head'), may hold values from -0.54 to 0.54
- key_input: float32 [16384, 4096], P('seq', 'head'), may hold values from -0.54 to 0.54
- value_input: float32 [16384, 4096], P('seq', 'head'), may hold values from -6 to 6
- grad_output: float32 [16384, 4096], P('seq', 'head'), may hold values from -0.54 to 0.54
- log_decay: float32 [16384, 32], P('seq', 'head'), may hold values from -2 to 0
- level_weight: float32 [16384, 7], P('seq'), may hold values from 0.3 to 1.5
- segment: int32 [16384], P('seq'), may hold values from 0 to 3, never falling along the last dimension, each value on 1 to 8192 neighbouring positions
Outputs:
- grad_query: float32 [16384, 4096], P('seq', 'head')
- grad_key: float32 [16384, 4096], P('seq', 'head')
- grad_value: float32 [16384, 4096], P('seq', 'head')
- grad_level: float32 [16384, 7], P('seq')
Inputs may be any that keep to these rules, and one draw needn't show every extreme that they name: `segment`: document numbers never fall along the tokens; each document has at most 8192 tokens, one exactly that many.
All inputs are finite; a program needn't handle non-finite values.
Results may differ from a plain program's by a relative error of at most 0.00012.
Values sent between devices are 32-bit elements; how exact they have to be, the bound alone decides.
A program may use at most 128 MiB of HBM per device.

v0:
```python
import jax
import jax.numpy as jnp
from jax import lax
from jax.experimental import pallas as pl
from jax.experimental.pallas import tpu as pltpu
from jax.sharding import PartitionSpec as P

F32 = jnp.float32
BF16 = jnp.bfloat16
NZ, NX = 8, 4
LV_ALL = 7
LV = 6


def split(a):
    hi = a.astype(BF16)
    return hi, (a - hi.astype(F32)).astype(BF16)


def left(a, axis):
    hi, lo = split(a)
    return jnp.concatenate([hi, hi, lo], axis=axis)


def right(a, axis):
    hi, lo = split(a)
    return jnp.concatenate([hi, lo, hi], axis=axis)


def mm(a, b, ca, cb):
    return lax.dot_general(a, b, (((ca,), (cb,)), ((), ())), preferred_element_type=F32)


def loop(n, fn):
    def body(i, carry):
        fn(i)
        return carry

    lax.fori_loop(0, n, body, 0)


def kernel(ldt, lwt, sgt, q_hbm, k_hbm, v_hbm, o_hbm, dq_hbm, dk_hbm, dv_hbm, glt,
           q, k, v, o, dq, dk, dv, packt,
           cumcol, ecol, swcol, lwcol, cumt, bias, bfac, gfac, pfac, lev,
           pb, zt, st, rf, tt, t01, rsb, zs, gs, gr, gx, rsg, gp, za, rz6, rz5, rz4, db,
           m3, r3, m2, r2, rl, ml, hb,
           s_in, s_out, s_g, r_g, s_1, r_1, s_rs, r_rs, s_x, r_x, s_z, r_z, s_ag, r_ag, s_f, r_f, s_p, r_p,
           s_bs, r_bs, s_bz, r_bz, s_d, r_d, s_m, r_m, s_b1, r_b1, s_h, r_h):
    n, heads, w = q.shape[0], swcol.shape[0], 128
    half = heads // 2
    me = lax.axis_index("seq")
    hd = lax.axis_index("head")
    nh = 4
    core = me % 2
    x = (me // 2) % NX
    z = me // (2 * NX)
    bits = [core, x % 2, x // 2, z % 2, (z // 2) % 2, z // 4]
    r0 = x * 2 + core

    def at(zz, xx, cc):
        return ((zz * NX + xx) * 2 + cc, hd)

    partner = at(z, x, 1 - core)

    def cp(src, dst, ss, rs, dev):
        return pltpu.make_async_remote_copy(
            src_ref=src, dst_ref=dst, send_sem=ss, recv_sem=rs,
            device_id=dev, device_id_type=pl.DeviceIdType.MESH)

    def bring(j):
        src, dst = ((k_hbm, k), (v_hbm, v), (o_hbm, o), (q_hbm, q))[j]
        return pltpu.make_async_copy(src, dst, s_in.at[j])

    for j in range(4):
        bring(j).start()

    barrier = pltpu.get_barrier_semaphore()
    plane_peers = [(d, e) for d in range(NX) for e in range(2) if (d, e) != (0, 0)]

    def plane_dev(d, e):
        return at(z, (x + d) % NX, (core + e) % 2)

    peers = [plane_dev(d, e) for d, e in plane_peers]
    peers += [at((z + d) % NZ, x, core) for d in range(1, NZ)]
    peers += [(me, (hd + d) % nh) for d in range(1, nh)]
    for dev in peers:
        pl.semaphore_signal(barrier, inc=1, device_id=dev, device_id_type=pl.DeviceIdType.MESH)

    packt[...] = jnp.zeros((w, n), F32)
    packt[0:heads, :] = ldt[...]
    packt[8:8 + LV_ALL, :] = lwt[...]
    packt[15:16, :] = sgt[...].astype(F32)
    pk = packt[...].T
    rows = lax.broadcasted_iota(jnp.int32, (n, n), 0)
    cols = lax.broadcasted_iota(jnp.int32, (n, n), 1)
    tri = (cols <= rows).astype(BF16)
    p1 = pk.astype(BF16)
    rest = pk - p1.astype(F32)
    p2 = rest.astype(BF16)
    p3 = (rest - p2.astype(F32)).astype(BF16)
    cum = mm(tri, p1, 1, 0) + mm(tri, p2, 1, 0) + mm(tri, p3, 1, 0)
    total = cum[n - 1:n, :]
    seg = pk[:, 15:16]
    own_end = pk[n - 1:n, 15:16]
    lane1 = lax.broadcasted_iota(jnp.int32, (1, w), 1)
    own_row = jnp.where(lane1 == heads, jnp.broadcast_to(own_end, (1, w)), total)
    pb[r0] = jnp.broadcast_to(own_row, (8, w))

    pl.semaphore_wait(barrier, len(peers))

    def g1(j):
        d, e = plane_peers[j]
        return cp(pb.at[r0], pb.at[r0], s_g.at[j], r_g.at[j], plane_dev(d, e))

    def g3(d):
        return cp(zt.at[z], zt.at[z], s_g.at[6 + d], r_g.at[6 + d], at((z + d) % NZ, x, core))

    for j in range(7):
        g1(j).start()
    sw = jnp.exp(total - cum) * (seg == own_end).astype(F32)
    for h in range(heads):
        swcol[h] = jnp.broadcast_to(sw[:, h:h + 1], (n, w))

    def own(i):
        return 2 * i + core

    def other(i):
        return 2 * i + 1 - core

    def f1_send(h):
        return cp(st.at[h], rf.at[0, h], s_1.at[h], r_1.at[h], partner)

    def head_cols(h):
        return pl.ds(pl.multiple_of(h * w, w), w)

    bring(0).wait()
    bring(1).wait()

    def make_state(h):
        vt = v[:, head_cols(h)].T
        st[h] = mm(left(vt, 1), right(k[:, head_cols(h)] * swcol[h], 0), 1, 0)

    def state_other(i):
        make_state(other(i))
        f1_send(other(i)).start()

    def state_own(i):
        make_state(own(i))

        @pl.when(core == 0)
        def _():
            f1_send(own(i)).start()

    loop(half, state_other)
    for j in range(7):
        g1(j).wait_recv()
    sub = lax.broadcasted_iota(jnp.int32, (8, w), 0)
    lane8 = lax.broadcasted_iota(jnp.int32, (8, w), 1)
    plane = jnp.zeros((8, w), F32)
    for r in range(8):
        plane = jnp.where(sub == r, pb[r], plane)
    zt[z] = plane
    for d in range(1, NZ):
        g3(d).start()

    def tools(tbl, idx):
        def row(c):
            return jnp.sum(jnp.where(idx == c, tbl, 0.0), axis=0, keepdims=True)

        def span(lo, hi):
            inside_span = jnp.where((idx > lo) & (idx <= hi), tbl, 0.0)
            return jnp.exp(jnp.minimum(jnp.sum(inside_span, axis=0, keepdims=True), 0.0))

        def same(a, b):
            return (row(a)[:, heads:heads + 1] == row(b)[:, heads:heads + 1]).astype(F32)

        return row, span, same

    def spread(vec):
        m = jnp.where(lane8 == sub, jnp.broadcast_to(vec, (8, w)), 0.0)
        return jnp.broadcast_to(jnp.sum(m, axis=1, keepdims=True), (8, w))

    row, span, same = tools(plane, sub)
    for l, low in ((0, 2 * x), (1, 4 * (x // 2) + 1)):
        up = low + (1 << l)
        bfac[l] = spread(span(low, up) * same(low, up))
    for j in range(NX):
        pfac[j] = spread(span(2 * j + 1, 7) * same(2 * j + 1, 7))

    def bf(l, h):
        return bfac[l, pl.ds(h, 1), :]

    def gf(l, h):
        return gfac[l, pl.ds(h, 1), :]

    def pf(j, h):
        return pfac[j, pl.ds(h, 1), :]

    loop(half, state_own)

    def f2_send(i):
        return cp(tt.at[i], rf.at[1, own(i)], s_x.at[0, i], r_x.at[0, i], at(z, (x + 1) % NX, core))

    def rs_send(d):
        i = (x + d) % NX
        return cp(tt.at[i], rsb.at[x], s_rs.at[d - 1], r_rs.at[d - 1], at(z, i, core))

    def rs_in(d):
        j = (x + NX - d) % NX
        return cp(tt.at[x], rsb.at[j], s_rs.at[d - 1], r_rs.at[d - 1], at(z, j, core))

    def f1(i):
        h = own(i)
        f1_send(h).wait_recv()
        b = bf(0, h)
        u = core == 1
        tt[i] = jnp.where(u, 1.0, b) * st[h] + jnp.where(u, b, 1.0) * rf[0, h]

    loop(half, f1)
    for d in (2, 1, 3):
        rs_send(d).start()

    @pl.when(x % 2 == 0)
    def _():
        loop(half, lambda i: f2_send(i).start())

    for h in range(heads):
        cumcol[h] = jnp.broadcast_to(cum[:, h:h + 1], (n, w))
    for l in range(LV_ALL):
        lwcol[l] = jnp.broadcast_to(pk[:, 8 + l:9 + l], (n, w))
    cumt[...] = cum.T
    segrow = packt[15:16, :]
    vis = (cols <= rows) & (jnp.broadcast_to(seg, (n, n)) == jnp.broadcast_to(segrow, (n, n)))
    bias[...] = jnp.where(vis, 0.0, -1e30)
    for l in range(LV_ALL):
        lev[l] = jnp.zeros((n, w), F32)

    for d in (1, 3, 2):
        rs_in(d).wait_recv()
    acc = pf(x, r0) * tt[x]
    for d in range(1, NX):
        j = (x + NX - d) % NX
        acc = acc + pf(j, r0) * rsb[j]
    zs[0] = acc

    def z4_send():
        return cp(zs.at[0], rf.at[3, r0], s_z.at[0], r_z.at[0], at((z + 1) % NZ, x, core))

    def z5_send(d):
        return cp(zs.at[1], rf.at[4, r0], s_z.at[d], r_z.at[1], at((z + d) % NZ, x, core))

    def z6_send(d):
        return cp(zs.at[2], rf.at[5, r0], s_z.at[2 + d], r_z.at[2], at((z + d) % NZ, x, core))

    @pl.when(z % 2 == 0)
    def _():
        z4_send().start()

    for d in range(1, NZ):
        g3(d).wait_recv()
    row, span, same = tools(zt[...].reshape(8 * NZ, w), lax.broadcasted_iota(jnp.int32, (8 * NZ, w), 0))
    for l in range(LV):
        hs = 1 << l
        low = (me // (2 * hs)) * (2 * hs) + hs - 1
        gfac[l] = spread(span(low, me - 1) * same(low, me - 1) * bits[l].astype(F32))
        if l in (3, 4):
            bfac[l] = spread(span(low, low + hs) * same(low, low + hs))
    prev_end = row(me - 1)[:, heads:heads + 1]
    ecum = jnp.exp(cum) * (seg == prev_end).astype(F32)
    for h in range(heads):
        ecol[h] = jnp.broadcast_to(ecum[:, h:h + 1], (n, w))

    def gp_send(l, i):
        return cp(gs.at[l, other(i)], gr.at[l - 1, i], s_p.at[l - 1, i], r_p.at[l - 1, i], partner)

    def make_g(h, l):
        lhs = left(o[:, head_cols(h)].T, 1)
        qe = q[:, head_cols(h)] * ecol[h]
        a = jnp.concatenate([qe * lwcol[l + 1], qe * lwcol[l + 2]], axis=1)
        both = mm(lhs, right(a, 0), 1, 0)
        gs[l, h] = both[:, :w] * gf(l, h)
        gs[l + 1, h] = both[:, w:] * gf(l + 1, h)

    def g_other(l):
        def one(i):
            make_g(other(i), l)
            for m in (l + 1, l):
                if m:
                    @pl.when(bits[m] == 1)
                    def _():
                        gp_send(m, i).start()

        return one

    def g_own(l):
        def one(i):
            make_g(own(i), l)

        return one

    def gsum(l, i):
        return gs[l, own(i)] + gr[l - 1, i]

    def bs_send(m, d):
        i = (x + d) % NX
        return cp(gx.at[m, i], rsg.at[m, x], s_bs.at[m, d - 1], r_bs.at[m, d - 1], at(z, i, core))

    def bs_in(m, d):
        j = (x + NX - d) % NX
        return cp(gx.at[m, x], rsg.at[m, j], s_bs.at[m, d - 1], r_bs.at[m, d - 1], at(z, j, core))

    def bs_out(m):
        @pl.when(bits[3 + m] == 1)
        def _():
            def one(i):
                gp_send(3 + m, i).wait_recv()
                gx[m, i] = gsum(3 + m, i)

            loop(half, one)
            for d in (2, 1, 3):
                bs_send(m, d).start()

    def bs_sum(m):
        for d in (1, 3, 2):
            bs_in(m, d).wait_recv()
        t = gx[m, x]
        for d in range(1, NX):
            t = t + rsg[m, (x + NX - d) % NX]
        gp[m] = t

    bring(2).wait()
    bring(3).wait()
    loop(half, g_other(4))
    loop(half, g_own(4))
    bs_out(2)

    @pl.when(z % 2 == 1)
    def _():
        z4_send().wait_recv()
        zs[1] = bf(3, r0) * rf[3, r0] + zs[0]

        @pl.when((z // 2) % 2 == 0)
        def _():
            z5_send(2).start()
            z5_send(1).start()

    loop(half, g_other(2))
    loop(half, g_own(2))
    bs_out(1)
    bs_out(0)

    @pl.when(z == 3)
    def _():
        z5_send(1).wait_recv()
        zs[2] = bf(4, r0) * rf[4, r0] + zs[1]
        for d in (4, 3, 2, 1):
            z6_send(d).start()

    def b6_send():
        return cp(gp.at[2], rz6.at[z % 4], s_bz.at[0], r_bz.at[z % 4], at(3, x, core))

    def b6_in(j):
        return cp(gp.at[2], rz6.at[j], s_bz.at[0], r_bz.at[j], at(4 + j, x, core))

    def b5_send():
        return cp(za.at[1], rz5.at[z % 2], s_bz.at[1], r_bz.at[4 + z % 2], at(4 * (z // 4) + 1, x, core))

    def b5_in(j):
        return cp(za.at[1], rz5.at[j], s_bz.at[1], r_bz.at[4 + j], at((z + 1 + j) % NZ, x, core))

    def b4_send():
        return cp(za.at[0], rz4, s_bz.at[2], r_bz.at[6], at((z + NZ - 1) % NZ, x, core))

    @pl.when(z >= 4)
    def _():
        bs_sum(2)
        b6_send().start()

    @pl.when(bits[4] == 1)
    def _():
        bs_sum(1)

        @pl.when(z != 3)
        def _():
            za[1] = gp[1]
            b5_send().start()

    @pl.when(z % 2 == 1)
    def _():
        bs_sum(0)

        @pl.when(z == 7)
        def _():
            za[0] = gp[0]
            b4_send().start()

    def ag_send(m, d):
        slot = rf.at[3 + m, r0]
        return cp(slot, slot, s_ag.at[m, d - 1], r_ag.at[m, d - 1], at(z, (x + d) % NX, core))

    def ag_in(m, d):
        slot = rf.at[3 + m, own((x + NX - d) % NX)]
        return cp(slot, slot, s_ag.at[m, d - 1], r_ag.at[m, d - 1], at(z, (x + NX - d) % NX, core))

    def fwd(l, i):
        slot = rf.at[l, own(i)]
        return cp(slot, slot, s_f.at[l - 1, i], r_f.at[l - 1, i], partner)

    def fwd_in(l, i):
        slot = rf.at[l, other(i)]
        return cp(slot, slot, s_f.at[l - 1, i], r_f.at[l - 1, i], partner)

    def hand_round(m):
        for d in (2, 1, 3):
            ag_send(m, d).start()
        fwd(3 + m, x).start()

    def hand_on(m):
        for d in (1, 3, 2):
            ag_in(m, d).wait_recv()
            fwd(3 + m, (x + NX - d) % NX).start()

    @pl.when(z % 2 == 1)
    def _():
        hand_round(0)

    @pl.when(bits[4] == 1)
    def _():
        @pl.when(z != 3)
        def _():
            z5_send(1).wait_recv()

        hand_round(1)

    def f3_send(src, i):
        return cp(src, rf.at[2, own(i)], s_x.at[1, i], r_x.at[1, i], at(z, (x + 1) % NX, core))

    @pl.when(x % 2 == 1)
    def _():
        def one(i):
            h = own(i)
            f2_send(i).wait_recv()
            fwd(1, i).start()

            @pl.when(x == 1)
            def _():
                t01[i] = bf(1, h) * rf[1, h] + tt[i]
                f3_send(t01.at[i], i).start()

        loop(half, one)

    loop(half, g_other(0))
    loop(half, g_own(0))

    def b3_send(i):
        return cp(m3.at[i], r3.at[i], s_m.at[0, i], r_m.at[0, i], at(z, (x + NX - 1) % NX, core))

    def b2_send(i):
        return cp(m2.at[i], r2.at[i], s_m.at[1, i], r_m.at[1, i], at(z, (x + NX - 1) % NX, core))

    @pl.when(x == 3)
    def _():
        def one(i):
            gp_send(2, i).wait_recv()
            m3[i] = gsum(2, i)
            b3_send(i).start()

        loop(half, one)

    def b1_early(i):
        return cp(gs.at[0, 2 * i], rl.at[2 * i], s_b1.at[i], r_b1.at[i], partner)

    @pl.when(core == 1)
    def _():
        loop(half, lambda i: b1_early(i).start())

    @pl.when(x == 2)
    def _():
        def one(i):
            f3_send(t01.at[i], i).wait_recv()
            f3_send(rf.at[2, own(i)], i).start()
            fwd(2, i).start()
            gp_send(2, i).wait_recv()
            b3_send(i).wait_recv()
            m3[i] = gsum(2, i) + r3[i]
            b3_send(i).start()

        loop(half, one)

    def inside(h):
        hc = head_cols(h)
        qh, kh, vh, oh = q[:, hc], k[:, hc], v[:, hc], o[:, hc]
        cc = cumcol[h]
        gap = jnp.concatenate([cc, cc], axis=1) - cumt[pl.ds(h, 1), :]
        within = jnp.exp(jnp.minimum(gap, 0.0) + bias[...])
        sc = mm(left(qh, 1), right(kh, 1), 1, 1)
        go = mm(left(oh, 1), right(vh, 1), 1, 1)
        lw = lwcol[0]
        wt = within * jnp.concatenate([lw, lw], axis=1)
        prod = within * sc * go
        lev[0] += prod[:, :w] + prod[:, w:]
        a = wt * sc
        b = wt * go
        dq[:, hc] = mm(left(b, 1), right(kh, 0), 1, 0)
        dv[:, hc] = mm(left(a.T, 1), right(oh, 0), 1, 0)
        dk[:, hc] = mm(left(b.T, 1), right(qh, 0), 1, 0)

    loop(half, inside)

    @pl.when(bits[3] == 1)
    def _():
        hand_on(0)

    @pl.when(bits[4] == 1)
    def _():
        hand_on(1)

    @pl.when(z == 3)
    def _():
        for j in range(4):
            b6_in(j).wait_recv()
        t = rz6[0] + rz6[1] + rz6[2] + rz6[3]
        za[1] = gp[1] + bf(4, r0) * t
        b5_send().start()
        za[0] = gp[0] + bf(3, r0) * t
        b4_send().start()
        db[x] = t

    @pl.when(z % 4 == 1)
    def _():
        for j in range(2):
            b5_in(j).wait_recv()
        t = rz5[0] + rz5[1]
        za[0] = gp[0] + bf(3, r0) * t
        b4_send().start()
        db[x] = t

    @pl.when(z == 7)
    def _():
        db[x] = jnp.zeros((w, w), F32)

    @pl.when(x % 2 == 1)
    def _():
        def one(i):
            gp_send(1, i).wait_recv()

            @pl.when(x == 1)
            def _():
                b3_send(i).wait_recv()
                m2[i] = gsum(1, i) + bf(1, own(i)) * r3[i]

            @pl.when(x == 3)
            def _():
                m2[i] = gsum(1, i)
                f3_send(t01.at[i], i).wait_recv()
                fwd(2, i).start()

            b2_send(i).start()

        loop(half, one)

    @pl.when(z >= 4)
    def _():
        z6_send(1).wait_recv()
        hand_round(2)

    @pl.when(z % 2 == 0)
    def _():
        b4_send().wait_recv()
        db[x] = rz4[...]

    def d_send(d):
        return cp(db.at[x], db.at[x], s_d.at[d - 1], r_d.at[d - 1], at(z, (x + d) % NX, core))

    def d_in(d):
        slot = db.at[(x + NX - d) % NX]
        return cp(slot, slot, s_d.at[d - 1], r_d.at[d - 1], at(z, (x + NX - d) % NX, core))

    for d in (2, 1, 3):
        d_send(d).start()
    loop(half, lambda i: inside(half + i))

    @pl.when(z >= 4)
    def _():
        hand_on(2)

    @pl.when(core == 1)
    def _():
        loop(half, lambda i: f1_send(2 * i).wait_recv())

    for l in range(1, 5):
        @pl.when(bits[l] == 1)
        def _():
            loop(half, lambda i: fwd_in(l, i).wait_recv())

    for d in (1, 3, 2):
        d_in(d).wait_recv()

    @pl.when(x % 2 == 0)
    def _():
        loop(half, lambda i: b2_send(i).wait_recv())

    def b1_up(i):
        return cp(ml.at[i], rl.at[own(i)], s_b1.at[half + i], r_b1.at[half + i], partner)

    def b1_up_in(i):
        return cp(ml.at[i], rl.at[other(i)], s_b1.at[half + i], r_b1.at[half + i], partner)

    def b1(i):
        h = own(i)
        t = pf(x, h) * db[i]
        extra = jnp.where(x == 1, r3[i], jnp.where(x == 3, 0.0, r2[i]))
        lam = t + extra

        @pl.when(core == 1)
        def _():
            ml[i] = bf(0, h) * lam + gs[0, h]
            rl[h] = lam

        @pl.when(core == 0)
        def _():
            ml[i] = lam
            b1_early(i).wait_recv()
            rl[h] = bf(0, h) * lam + rl[h]

        b1_up(i).start()

    loop(half, b1)

    def put(j, h):
        src, dst = ((dq, dq_hbm), (dk, dk_hbm), (dv, dv_hbm))[j]
        hc = head_cols(h)
        return pltpu.make_async_copy(src.at[:, hc], dst.at[:, hc], s_out.at[j, h])

    @pl.when(bits[5] == 1)
    def _():
        loop(half, lambda i: fwd_in(5, i).wait_recv())

    def levels(h):
        hc = head_cols(h)
        oh = left(o[:, hc], 1)
        qh = q[:, hc]
        e = ecol[h]
        acc = dq[:, hc]
        for l in range(0, LV, 2):
            pair = []
            for m in (l, l + 1):
                pair.append(jnp.where(bits[m] == 1, rf[m, h] * gf(m, h), 0.0))
            back = mm(oh, right(jnp.concatenate(pair, axis=1), 0), 1, 0)
            for m in (l, l + 1):
                part = e * back[:, (m - l) * w:(m - l + 1) * w]
                lev[m + 1] += qh * part
                acc = acc + lwcol[m + 1] * part
        dq[:, hc] = acc
        put(0, h).start()

    def sources(h):
        hc = head_cols(h)
        g = rl[h]
        s = swcol[h]
        dk[:, hc] += s * mm(left(v[:, hc], 1), right(g, 0), 1, 0)
        put(1, h).start()
        dv[:, hc] += s * mm(left(k[:, hc], 1), right(g, 1), 1, 1)
        put(2, h).start()

    loop(heads, levels)

    lanes = lax.broadcasted_iota(jnp.int32, (n, w), 1)
    acc = jnp.zeros((n, w), F32)
    for l in range(LV_ALL):
        acc = jnp.where(lanes == l, jnp.sum(lev[l], axis=1, keepdims=True), acc)
    hb[hd] = acc.T[:8, :]

    def h_send(d):
        return cp(hb.at[hd], hb.at[hd], s_h.at[d - 1], r_h.at[d - 1], (me, (hd + d) % nh))

    for d in range(1, nh):
        h_send(d).start()
    loop(half, lambda i: b1_up_in(i).wait_recv())
    loop(heads, sources)
    for d in range(1, nh):
        h_send(d).wait_recv()
    tot = hb[0] + hb[1] + hb[2] + hb[3]
    glt[...] = tot[:LV_ALL, :]

    for j in range(3):
        loop(heads, lambda h: put(j, h).wait())
    for d in range(1, nh):
        h_send(d).wait_send()
    for j in range(7):
        g1(j).wait_send()
    for d in range(1, NZ):
        g3(d).wait_send()
    loop(half, lambda i: f1_send(other(i)).wait_send())

    @pl.when(core == 0)
    def _():
        loop(half, lambda i: f1_send(own(i)).wait_send())

    @pl.when(core == 1)
    def _():
        loop(half, lambda i: b1_early(i).wait_send())

    for d in range(1, NX):
        rs_send(d).wait_send()
        d_send(d).wait_send()

    @pl.when(x % 2 == 0)
    def _():
        loop(half, lambda i: f2_send(i).wait_send())

    @pl.when((x == 1) | (x == 2))
    def _():
        loop(half, lambda i: f3_send(t01.at[i], i).wait_send())

    @pl.when(x >= 2)
    def _():
        loop(half, lambda i: b3_send(i).wait_send())

    @pl.when(x % 2 == 1)
    def _():
        loop(half, lambda i: b2_send(i).wait_send())

    loop(half, lambda i: b1_up(i).wait_send())
    for l in range(1, LV):
        @pl.when(bits[l] == 1)
        def _():
            loop(half, lambda i: fwd(l, i).wait_send())
            loop(half, lambda i: gp_send(l, i).wait_send())

    for m in range(3):
        @pl.when(bits[3 + m] == 1)
        def _():
            for d in range(1, NX):
                bs_send(m, d).wait_send()
                ag_send(m, d).wait_send()

    @pl.when(z % 2 == 0)
    def _():
        z4_send().wait_send()

    @pl.when(z % 4 == 1)
    def _():
        z5_send(1).wait_send()
        z5_send(2).wait_send()

    @pl.when(z == 3)
    def _():
        for d in range(1, 5):
            z6_send(d).wait_send()

    @pl.when(z >= 4)
    def _():
        b6_send().wait_send()

    @pl.when(bits[4] == 1)
    def _():
        b5_send().wait_send()

    @pl.when(z % 2 == 1)
    def _():
        b4_send().wait_send()


def on_device(queries, key_input, value_input, grad_output, log_decay, level_weight, segment):
    n, heads = log_decay.shape
    width = queries.shape[1]
    w = 128
    half = heads // 2
    dma = pltpu.SemaphoreType.DMA

    def mem(*shape):
        return pltpu.VMEM(shape, F32)

    scratch = [mem(n, width) for _ in range(7)] + [mem(w, n)]
    scratch += [mem(heads, n, w), mem(heads, n, w), mem(heads, n, w), mem(LV_ALL, n, w),
                mem(w, n), mem(n, n), mem(LV, 8, w), mem(LV, 8, w), mem(NX, 8, w), mem(LV_ALL, n, w)]
    scratch += [mem(8, 8, w), mem(NZ, 8, w), mem(heads, w, w), mem(LV, heads, w, w),
                mem(half, w, w), mem(half, w, w), mem(NX, w, w), mem(3, w, w),
                mem(LV, heads, w, w), mem(LV - 1, half, w, w), mem(3, half, w, w), mem(3, NX, w, w),
                mem(3, w, w), mem(2, w, w), mem(4, w, w), mem(2, w, w), mem(w, w), mem(NX, w, w)]
    scratch += [mem(half, w, w) for _ in range(4)] + [mem(heads, w, w), mem(half, w, w), mem(4, 8, n)]
    scratch += [dma((4,)), dma((3, heads))]
    for a, b in (((14,), (14,)), ((heads,), (heads,)), ((3,), (3,)), ((2, half), (2, half)), ((7,), (3,)),
                 ((3, 3), (3, 3)), ((LV - 1, half), (LV - 1, half)), ((LV - 1, half), (LV - 1, half)),
                 ((3, 3), (3, 3)), ((3,), (7,)), ((3,), (3,)), ((2, half), (2, half)),
                 ((heads,), (heads,)), ((3,), (3,))):
        scratch += [dma(a), dma(b)]
    vm = pl.BlockSpec(memory_space=pltpu.VMEM)
    hbm = pl.BlockSpec(memory_space=pl.ANY)
    out = jax.ShapeDtypeStruct((n, width), F32)
    dq, dk, dv, glt = pl.pallas_call(
        kernel,
        out_shape=(out, out, out, jax.ShapeDtypeStruct((LV_ALL, n), F32)),
        in_specs=[vm] * 3 + [hbm] * 4,
        out_specs=(hbm, hbm, hbm, vm),
        scratch_shapes=scratch,
        compiler_params=pltpu.CompilerParams(
            collective_id=0, has_side_effects=True, vmem_limit_bytes=60 << 20),
    )(log_decay.T, level_weight.T, segment[None, :], queries, key_input, value_input, grad_output)
    return dq, dk, dv, glt.T


def solution(mesh):
    in_specs = (
        P("seq", "head"),
        P("seq", "head"),
        P("seq", "head"),
        P("seq", "head"),
        P("seq", "head"),
        P("seq", None),
        P("seq"),
    )
    out_specs = (P("seq", "head"), P("seq", "head"), P("seq", "head"), P("seq", None))
    return jax.shard_map(
        on_device, mesh=mesh, in_specs=in_specs, out_specs=out_specs, check_vma=False
    )
```

profile of v0, /device:TPU:8, one launch (start us, length us, event | category | flops | bytes accessed | tf_op | source)
XLA Modules:
  0.0 77.5 jit_solution(7406033000368466462)
XLA Ops:
  0.6 71.3 %shard_map.102 = (f32[256,1024]{1,0:T(8,128)}, f32[256,1024]{1,0:T(8,128)}, f32[256,1024]{1,0:T(8,128)}, f32[7,256]{1,0:T(8,128)}) custom-call(f32[8,256]{1,0:T(8,128)} %bitcast.4, f32[7,256]{1,0:T(8,128)} %bitcast.5, s32[1,256]{1,0:T(1,128)} %bitcast.7, f32[256,1024]{1,0:T(8,128)} %q_hbm.1, f32[256,1024]{1,0:T(8,128)} %k_hbm.1, f32[256,1024]{1,0:T(8,128)} %v_hbm.1, ...), custom_call_target="tpu_custom_call" | custom-call | tf_op jit(solution)/shard_map/pallas_call | solution.py:792
  71.9 0.0 copy-start.1
  71.9 2.4 %copy.15 = f32[256,1024]{1,0:T(8,128)} copy(f32[256,1024]{1,0:T(8,128)} %get-tuple-element.16) | data formatting | bytes 2097152
  74.3 0.0 copy-done.1
  74.3 0.0 copy-start
  74.3 1.0 %copy.16 = f32[256,1024]{1,0:T(8,128)} copy(f32[256,1024]{1,0:T(8,128)S(1)} %copy-done.1) | data formatting | bytes 2097152
  75.3 0.6 copy-done
  76.0 0.0 copy-start.2
  76.0 1.0 %copy.17 = f32[256,1024]{1,0:T(8,128)} copy(f32[256,1024]{1,0:T(8,128)S(1)} %copy-done) | data formatting | bytes 2097152
  76.9 0.0 copy-done.2
  76.9 0.6 copy.18
Async XLA Ops:
  71.9 2.4 %copy-start.1 = (f32[256,1024]{1,0:T(8,128)S(1)}, f32[256,1024]{1,0:T(8,128)}, u32[]{:S(2)}) copy-start(f32[256,1024]{1,0:T(8,128)} %get-tuple-element.17) | copy-start | bytes 3145732
  74.3 1.6 %copy-start = (f32[256,1024]{1,0:T(8,128)S(1)}, f32[256,1024]{1,0:T(8,128)}, u32[]{:S(2)}) copy-start(f32[256,1024]{1,0:T(8,128)} %get-tuple-element.18) | copy-start | bytes 3145732
  76.0 1.0 %copy-start.2 = (f32[7,256]{1,0:T(8,128)S(1)}, f32[7,256]{1,0:T(8,128)}, u32[]{:S(2)}) copy-start(f32[7,256]{1,0:T(8,128)} %get-tuple-element.11) | copy-start | bytes 21508
where the time goes:
time: 77.7 us; the launch traced here: 77.5 us
  Pallas kernels  71.3 us (92%)
  local copies, waits for them, and re-layouts  5.57 us (7%)
    pallas_call x1, Pallas kernels, on_device(): pl.pallas_call(kernel, out_shape=(out, out, out, jax.ShapeDtypeStruct((LV...  71.3 us
    unnamed x10, local copies, waits for them, and re-layouts  5.57 us

commit v1 on v0

v1 whole, which is shorter than its diff:
```python
import jax
import jax.numpy as jnp
from jax import lax
from jax.experimental import pallas as pl
from jax.experimental.pallas import tpu as pltpu
from jax.sharding import PartitionSpec as P

F32 = jnp.float32
BF16 = jnp.bfloat16
NZ, NX = 8, 4
LV_ALL = 7
LV = 6


def split(a):
    hi = a.astype(BF16)
    return hi, (a - hi.astype(F32)).astype(BF16)


def left(a, axis):
    hi, lo = split(a)
    return jnp.concatenate([hi, hi, lo], axis=axis)


def right(a, axis):
    hi, lo = split(a)
    return jnp.concatenate([hi, lo, hi], axis=axis)


def mm(a, b, ca, cb):
    return lax.dot_general(a, b, (((ca,), (cb,)), ((), ())), preferred_element_type=F32)


def loop(n, fn):
    def body(i, carry):
        fn(i)
        return carry

    lax.fori_loop(0, n, body, 0)


def kernel(ldt, lwt, sgt, q_hbm, k_hbm, v_hbm, o_hbm, dq_hbm, dk_hbm, dv_hbm, glt,
           q, k, v, o, dq, dk, dv, packt,
           cumcol, ecol, swcol, lwcol, cumt, bias, bfac, gfac, hfac, pfac, lev,
           pb, zt, st, rf, tt, t01, rsb, zs, gs, gr, gx, rsg, gp, za, rz6, rz5, rz4, db,
           gxx, rsx, lo, dp, ge, rl, ml, hb, olhs,
           s_in, s_out, s_g, r_g, s_1, r_1, s_rs, r_rs, s_x, r_x, s_z, r_z, s_ag, r_ag, s_f, r_f, s_p, r_p,
           s_bs, r_bs, s_bz, r_bz, s_d, r_d, s_m, r_m, s_b1, r_b1, s_h, r_h):
    n, heads, w = q.shape[0], swcol.shape[0], 128
    half = heads // 2
    me = lax.axis_index("seq")
    hd = lax.axis_index("head")
    nh = 4
    core = me % 2
    x = (me // 2) % NX
    z = me // (2 * NX)
    bits = [core, x % 2, x // 2, z % 2, (z // 2) % 2, z // 4]
    r0 = x * 2 + core

    def at(zz, xx, cc):
        return ((zz * NX + xx) * 2 + cc, hd)

    partner = at(z, x, 1 - core)

    def cp(src, dst, ss, rs, dev):
        return pltpu.make_async_remote_copy(
            src_ref=src, dst_ref=dst, send_sem=ss, recv_sem=rs,
            device_id=dev, device_id_type=pl.DeviceIdType.MESH)

    def bring(j):
        src, dst = ((k_hbm, k), (v_hbm, v), (o_hbm, o), (q_hbm, q))[j]
        return pltpu.make_async_copy(src, dst, s_in.at[j])

    for j in range(4):
        bring(j).start()

    barrier = pltpu.get_barrier_semaphore()
    plane_peers = [(d, e) for d in range(NX) for e in range(2) if (d, e) != (0, 0)]

    def plane_dev(d, e):
        return at(z, (x + d) % NX, (core + e) % 2)

    peers = [plane_dev(d, e) for d, e in plane_peers]
    peers += [at((z + d) % NZ, x, core) for d in range(1, NZ)]
    peers += [(me, (hd + d) % nh) for d in range(1, nh)]
    for dev in peers:
        pl.semaphore_signal(barrier, inc=1, device_id=dev, device_id_type=pl.DeviceIdType.MESH)

    packt[...] = jnp.zeros((w, n), F32)
    packt[0:heads, :] = ldt[...]
    packt[8:8 + LV_ALL, :] = lwt[...]
    packt[15:16, :] = sgt[...].astype(F32)
    pk = packt[...].T
    rows = lax.broadcasted_iota(jnp.int32, (n, n), 0)
    cols = lax.broadcasted_iota(jnp.int32, (n, n), 1)
    tri = (cols <= rows).astype(BF16)
    p1 = pk.astype(BF16)
    rest = pk - p1.astype(F32)
    p2 = rest.astype(BF16)
    p3 = (rest - p2.astype(F32)).astype(BF16)
    cum = mm(tri, p1, 1, 0) + mm(tri, p2, 1, 0) + mm(tri, p3, 1, 0)
    total = cum[n - 1:n, :]
    seg = pk[:, 15:16]
    own_end = pk[n - 1:n, 15:16]
    lane1 = lax.broadcasted_iota(jnp.int32, (1, w), 1)
    own_row = jnp.where(lane1 == heads, jnp.broadcast_to(own_end, (1, w)), total)
    own_row = jnp.where(lane1 == heads + 1, jnp.broadcast_to(pk[0:1, 15:16], (1, w)), own_row)
    pb[r0] = jnp.broadcast_to(own_row, (8, w))

    pl.semaphore_wait(barrier, len(peers))

    def g1(j):
        d, e = plane_peers[j]
        return cp(pb.at[r0], pb.at[r0], s_g.at[j], r_g.at[j], plane_dev(d, e))

    def g3(d):
        return cp(zt.at[z], zt.at[z], s_g.at[6 + d], r_g.at[6 + d], at((z + d) % NZ, x, core))

    for j in range(7):
        g1(j).start()
    sw = jnp.exp(total - cum) * (seg == own_end).astype(F32)
    for h in range(heads):
        swcol[h] = jnp.broadcast_to(sw[:, h:h + 1], (n, w))

    def own(i):
        return 2 * i + core

    def other(i):
        return 2 * i + 1 - core

    def f1_send(h):
        return cp(st.at[h], rf.at[0, h], s_1.at[h], r_1.at[h], partner)

    def head_cols(h):
        return pl.ds(pl.multiple_of(h * w, w), w)

    bring(0).wait()
    bring(1).wait()

    def make_state(h):
        vt = v[:, head_cols(h)].T
        st[h] = mm(left(vt, 1), right(k[:, head_cols(h)] * swcol[h], 0), 1, 0)

    def state_other(i):
        make_state(other(i))
        f1_send(other(i)).start()

    def state_own(i):
        make_state(own(i))

        @pl.when(core == 0)
        def _():
            f1_send(own(i)).start()

    loop(half, state_other)
    loop(half, state_own)
    first = pk[0:1, 15:16]
    ecum = jnp.exp(cum) * (seg == first).astype(F32)
    for h in range(heads):
        ecol[h] = jnp.broadcast_to(ecum[:, h:h + 1], (n, w))
    for l in range(LV_ALL):
        lwcol[l] = jnp.broadcast_to(pk[:, 8 + l:9 + l], (n, w))

    def gp_send(l, i):
        return cp(gs.at[l, other(i)], gr.at[l - 1, i], s_p.at[l - 1, i], r_p.at[l - 1, i], partner)

    def make_g(h, l):
        if l == 4:
            olhs[h] = left(o[:, head_cols(h)].T, 1)
        lhs = olhs[h]
        qe = q[:, head_cols(h)] * ecol[h]
        a = jnp.concatenate([qe * lwcol[l + 1], qe * lwcol[l + 2]], axis=1)
        both = mm(lhs, right(a, 0), 1, 0)
        gs[l, h] = both[:, :w]
        gs[l + 1, h] = both[:, w:]

    def g_other(l):
        def one(i):
            make_g(other(i), l)
            for m in (l + 1, l):
                if m:
                    @pl.when(bits[m] == 1)
                    def _():
                        gp_send(m, i).start()

        return one

    def g_own(l):
        def one(i):
            make_g(own(i), l)

        return one

    bring(2).wait()
    bring(3).wait()
    loop(half, g_other(4))
    for j in range(7):
        g1(j).wait_recv()
    sub = lax.broadcasted_iota(jnp.int32, (8, w), 0)
    lane8 = lax.broadcasted_iota(jnp.int32, (8, w), 1)
    plane = jnp.zeros((8, w), F32)
    for r in range(8):
        plane = jnp.where(sub == r, pb[r], plane)
    zt[z] = plane
    for d in range(1, NZ):
        g3(d).start()

    def tools(tbl, idx):
        def row(c):
            return jnp.sum(jnp.where(idx == c, tbl, 0.0), axis=0, keepdims=True)

        def span(lo, hi):
            inside_span = jnp.where((idx > lo) & (idx <= hi), tbl, 0.0)
            return jnp.exp(jnp.minimum(jnp.sum(inside_span, axis=0, keepdims=True), 0.0))

        def same(a, b):
            return (row(a)[:, heads:heads + 1] == row(b)[:, heads:heads + 1]).astype(F32)

        return row, span, same

    def spread(vec):
        m = jnp.where(lane8 == sub, jnp.broadcast_to(vec, (8, w)), 0.0)
        return jnp.broadcast_to(jnp.sum(m, axis=1, keepdims=True), (8, w))

    row, span, same = tools(plane, sub)
    for l, low in ((0, 2 * x), (1, 1)):
        up = low + (1 << l)
        bfac[l] = spread(span(low, up) * same(low, up))
    for j in range(NX):
        pfac[j] = spread(span(2 * j + 1, 7) * same(2 * j + 1, 7))

    def bf(l, h):
        return bfac[l, pl.ds(h, 1), :]

    def gf(l, h):
        return gfac[l, pl.ds(h, 1), :]

    def pf(j, h):
        return pfac[j, pl.ds(h, 1), :]

    def rs_send(d):
        i = (x + d) % NX
        return cp(tt.at[i], rsb.at[x], s_rs.at[d - 1], r_rs.at[d - 1], at(z, i, core))

    def rs_in(d):
        j = (x + NX - d) % NX
        return cp(tt.at[x], rsb.at[j], s_rs.at[d - 1], r_rs.at[d - 1], at(z, j, core))

    def f1(i):
        h = own(i)
        f1_send(h).wait_recv()
        b = bf(0, h)
        u = core == 1
        tt[i] = jnp.where(u, 1.0, b) * st[h] + jnp.where(u, b, 1.0) * rf[0, h]

    loop(half, f1)
    for d in (2, 1, 3):
        rs_send(d).start()

    loop(half, g_own(4))
    loop(half, g_other(2))
    for h in range(heads):
        cumcol[h] = jnp.broadcast_to(cum[:, h:h + 1], (n, w))
    cumt[...] = cum.T
    segrow = packt[15:16, :]
    vis = (cols <= rows) & (jnp.broadcast_to(seg, (n, n)) == jnp.broadcast_to(segrow, (n, n)))
    bias[...] = jnp.where(vis, 0.0, -1e30)
    for l in range(LV_ALL):
        lev[l] = jnp.zeros((n, w), F32)

    loop(half, g_own(2))

    for d in (1, 3, 2):
        rs_in(d).wait_recv()
    rsb[x] = tt[x]
    acc = pf(0, r0) * rsb[0]
    for j in range(1, NX):
        acc = acc + pf(j, r0) * rsb[j]
    zs[0] = acc

    def z4_send():
        return cp(zs.at[0], rf.at[3, r0], s_z.at[0], r_z.at[0], at((z + 1) % NZ, x, core))

    def z5_send(d):
        return cp(zs.at[1], rf.at[4, r0], s_z.at[d], r_z.at[1], at((z + d) % NZ, x, core))

    def z6_send(d):
        return cp(zs.at[2], rf.at[5, r0], s_z.at[2 + d], r_z.at[2], at((z + d) % NZ, x, core))

    @pl.when(z % 2 == 0)
    def _():
        z4_send().start()

    for d in range(1, NZ):
        g3(d).wait_recv()
    row, span, same = tools(zt[...].reshape(8 * NZ, w), lax.broadcasted_iota(jnp.int32, (8 * NZ, w), 0))
    def starts(r):
        c = z * 2 * NX + r
        return (row(c)[:, heads + 1:heads + 2] == row(c - 1)[:, heads:heads + 1]).astype(F32)

    for l in range(LV):
        hs = 1 << l
        low = (me // (2 * hs)) * (2 * hs) + hs - 1
        prev = me - 1
        gfac[l] = spread(span(low, prev) * same(low, prev) * starts(r0) * bits[l].astype(F32))
        if l:
            other_prev = me - 2 * core
            hfac[l] = spread(span(low, other_prev) * same(low, other_prev) * starts(r0 + 1 - 2 * core) * bits[l].astype(F32))
        if l in (3, 4):
            bfac[l] = spread(span(low, low + hs) * same(low, low + hs))
    def gsum(l, i):
        return gs[l, own(i)] * gf(l, own(i)) + gr[l - 1, i] * hfac[l, pl.ds(own(i), 1), :]

    def bs_send(m, d):
        i = (x + d) % NX
        return cp(gx.at[m, i], rsg.at[m, x], s_bs.at[m, d - 1], r_bs.at[m, d - 1], at(z, i, core))

    def bs_in(m, d):
        j = (x + NX - d) % NX
        return cp(gx.at[m, x], rsg.at[m, j], s_bs.at[m, d - 1], r_bs.at[m, d - 1], at(z, j, core))

    def bs_out(m):
        @pl.when(bits[3 + m] == 1)
        def _():
            def one(i):
                gp_send(3 + m, i).wait_recv()
                gx[m, i] = gsum(3 + m, i)

            loop(half, one)
            for d in (2, 1, 3):
                bs_send(m, d).start()

    def bs_sum(m):
        for d in (1, 3, 2):
            bs_in(m, d).wait_recv()
        t = gx[m, x]
        for d in range(1, NX):
            t = t + rsg[m, (x + NX - d) % NX]
        gp[m] = t

    bs_out(2)
    bs_out(1)
    bs_out(0)
    loop(half, g_other(0))
    loop(half, g_own(0))

    def ag_send(m, d):
        slot = rf.at[3 + m, r0]
        return cp(slot, slot, s_ag.at[m, d - 1], r_ag.at[m, d - 1], at(z, (x + d) % NX, core))

    def ag_in(m, d):
        slot = rf.at[3 + m, own((x + NX - d) % NX)]
        return cp(slot, slot, s_ag.at[m, d - 1], r_ag.at[m, d - 1], at(z, (x + NX - d) % NX, core))

    def fwd(l, i):
        slot = rf.at[l, own(i)]
        return cp(slot, slot, s_f.at[l - 1, i], r_f.at[l - 1, i], partner)

    def fwd_in(l, i):
        slot = rf.at[l, other(i)]
        return cp(slot, slot, s_f.at[l - 1, i], r_f.at[l - 1, i], partner)

    def hand_round(m):
        for d in (2, 1, 3):
            ag_send(m, d).start()
        fwd(3 + m, x).start()

    def hand_on(m):
        for d in (1, 3, 2):
            ag_in(m, d).wait_recv()
            fwd(3 + m, (x + NX - d) % NX).start()

    @pl.when(z % 2 == 1)
    def _():
        z4_send().wait_recv()
        zs[1] = bf(3, r0) * rf[3, r0] + zs[0]

        @pl.when((z // 2) % 2 == 0)
        def _():
            z5_send(2).start()
            z5_send(1).start()

    @pl.when(z % 2 == 1)
    def _():
        hand_round(0)

    def bx_send(c, l, d):
        i = (x + d) % NX
        return cp(gxx.at[l - 1, i], rsx.at[c], s_m.at[l - 1, d - 1], r_m.at[c], at(z, i, core))

    def bx_in(c, l):
        return cp(gxx.at[l - 1, x], rsx.at[c], s_m.at[l - 1, 0], r_m.at[c], at(z, x, 1 - core))

    b_plan = ((1, 1), (3, 1), (2, 2), (3, 2))
    for c in (2, 3, 0, 1):
        frm, l = b_plan[c]

        @pl.when(x == frm)
        def _():
            def one(i):
                gp_send(l, i).wait_recv()
                gxx[l - 1, i] = gsum(l, i)

            loop(half, one)
            rsx[c] = gxx[l - 1, x]
            for d in (2, 1, 3):
                bx_send(c, l, d).start()

    t01[...] = bf(1, r0) * rsb[0] + rsb[1]
    x_plan = ((1, 1, 0), (3, 1, 2), (2, 2, None), (3, 2, None))

    def fx_send(c):
        to, l, j = x_plan[c]
        src = t01 if j is None else rsb.at[j]
        return cp(src, rf.at[l, r0], s_x.at[c], r_x.at[l - 1, (to + NX - x + 3) % NX], at(z, to, core))

    def fx_in(l, d):
        j = (x + NX - d) % NX
        return cp(t01, rf.at[l, own(j)], s_x.at[0], r_x.at[l - 1, d - 1], at(z, j, core))

    for c in range(4):
        to, l, j = x_plan[c]

        @pl.when(x == to)
        def _():
            rf[l, r0] = t01[...] if j is None else rsb[j]

        @pl.when(x != to)
        def _():
            fx_send(c).start()

    def b6_send():
        return cp(gp.at[2], rz6.at[z % 4], s_bz.at[0], r_bz.at[z % 4], at(3, x, core))

    def b6_in(j):
        return cp(gp.at[2], rz6.at[j], s_bz.at[0], r_bz.at[j], at(4 + j, x, core))

    def b5_send():
        return cp(za.at[1], rz5.at[z % 2], s_bz.at[1], r_bz.at[4 + z % 2], at(4 * (z // 4) + 1, x, core))

    def b5_in(j):
        return cp(za.at[1], rz5.at[j], s_bz.at[1], r_bz.at[4 + j], at((z + 1 + j) % NZ, x, core))

    def b4_send():
        return cp(za.at[0], rz4, s_bz.at[2], r_bz.at[6], at((z + NZ - 1) % NZ, x, core))

    @pl.when(z >= 4)
    def _():
        bs_sum(2)
        b6_send().start()

    @pl.when(z == 3)
    def _():
        z5_send(1).wait_recv()
        zs[2] = bf(4, r0) * rf[4, r0] + zs[1]
        for d in (4, 3, 2, 1):
            z6_send(d).start()

    @pl.when(bits[4] == 1)
    def _():
        @pl.when(z != 3)
        def _():
            z5_send(1).wait_recv()

        hand_round(1)

    def b1_early(i):
        return cp(ge.at[i], rl.at[2 * i], s_b1.at[i], r_b1.at[i], partner)

    @pl.when(core == 1)
    def _():
        def one(i):
            ge[i] = gs[0, 2 * i] * gf(0, 2 * i)
            b1_early(i).start()

        loop(half, one)

    def inside(h):
        hc = head_cols(h)
        qh, kh, vh, oh = q[:, hc], k[:, hc], v[:, hc], o[:, hc]
        cc = cumcol[h]
        gap = jnp.concatenate([cc, cc], axis=1) - cumt[pl.ds(h, 1), :]
        within = jnp.exp(jnp.minimum(gap, 0.0) + bias[...])
        sc = mm(left(qh, 1), right(kh, 1), 1, 1)
        go = mm(left(oh, 1), right(vh, 1), 1, 1)
        lw = lwcol[0]
        wt = within * jnp.concatenate([lw, lw], axis=1)
        prod = within * sc * go
        lev[0] += prod[:, :w] + prod[:, w:]
        a = wt * sc
        b = wt * go
        dq[:, hc] = mm(left(b, 1), right(kh, 0), 1, 0)
        dv[:, hc] = mm(left(a.T, 1), right(oh, 0), 1, 0)
        dk[:, hc] = mm(left(b.T, 1), right(qh, 0), 1, 0)

    def d_send(d):
        return cp(lo.at[(x + d) % NX], db.at[x], s_d.at[d - 1], r_d.at[d - 1], at(z, (x + d) % NX, core))

    def d_in(d):
        return cp(lo.at[x], db.at[(x + NX - d) % NX], s_d.at[d - 1], r_d.at[d - 1], at(z, (x + NX - d) % NX, core))

    def b1_up(i):
        return cp(ml.at[i], rl.at[own(i)], s_b1.at[half + i], r_b1.at[half + i], partner)

    def b1_up_in(i):
        return cp(ml.at[i], rl.at[other(i)], s_b1.at[half + i], r_b1.at[half + i], partner)

    def b1(i):
        h = own(i)
        lam = db[i]

        @pl.when(core == 1)
        def _():
            ml[i] = bf(0, h) * lam + gs[0, h] * gf(0, h)
            rl[h] = lam

        @pl.when(core == 0)
        def _():
            ml[i] = lam
            b1_early(i).wait_recv()
            rl[h] = bf(0, h) * lam + rl[h]

        b1_up(i).start()

    def put(j, h):
        src, dst = ((dq, dq_hbm), (dk, dk_hbm), (dv, dv_hbm))[j]
        hc = head_cols(h)
        return pltpu.make_async_copy(src.at[:, hc], dst.at[:, hc], s_out.at[j, h])

    def levels(pairs, last):
        def one(h):
            hc = head_cols(h)
            oh = left(o[:, hc], 1)
            qh = q[:, hc]
            e = ecol[h]
            acc = dq[:, hc]
            for l in pairs:
                pair = []
                for m in (l, l + 1):
                    pair.append(jnp.where(bits[m] == 1, rf[m, h] * gf(m, h), 0.0))
                back = mm(oh, right(jnp.concatenate(pair, axis=1), 0), 1, 0)
                for m in (l, l + 1):
                    part = e * back[:, (m - l) * w:(m - l + 1) * w]
                    lev[m + 1] += qh * part
                    acc = acc + lwcol[m + 1] * part
            dq[:, hc] = acc
            if last:
                put(0, h).start()

        loop(heads, one)

    def sources(h):
        hc = head_cols(h)
        g = rl[h]
        s = swcol[h]
        dk[:, hc] += s * mm(left(v[:, hc], 1), right(g, 0), 1, 0)
        put(1, h).start()
        dv[:, hc] += s * mm(left(k[:, hc], 1), right(g, 1), 1, 1)
        put(2, h).start()

    def h_send(d):
        return cp(hb.at[hd], hb.at[hd], s_h.at[d - 1], r_h.at[d - 1], (me, (hd + d) % nh))

    def level_sums():
        lanes = lax.broadcasted_iota(jnp.int32, (n, w), 1)
        acc = jnp.zeros((n, w), F32)
        for l in range(LV_ALL):
            acc = jnp.where(lanes == l, jnp.sum(lev[l], axis=1, keepdims=True), acc)
        hb[hd] = acc.T[:8, :]
        for d in range(1, nh):
            h_send(d).start()

    def x_blocks():
        def fx_all(l):
            fwd(l, x).start()
            for d in (1, 3, 2):
                fx_in(l, d).wait_recv()
                fwd(l, (x + NX - d) % NX).start()

        @pl.when(x % 2 == 1)
        def _():
            fx_all(1)

        @pl.when(x >= 2)
        def _():
            fx_all(2)

    def from_partner(levels_in):
        for l in levels_in:
            @pl.when(bits[l] == 1)
            def _():
                loop(half, lambda i: fwd_in(l, i).wait_recv())

    def plane_gradient():
        @pl.when(z % 2 == 0)
        def _():
            b4_send().wait_recv()
            dp[...] = rz4[...]

        for c in range(4):
            frm, l = b_plan[c]

            @pl.when(x != frm)
            def _():
                bx_in(c, l).wait_recv()

        t = dp[...]
        both = rsx[2] + rsx[3]
        lo[0] = pf(0, r0) * t + rsx[0] + bf(1, r0) * both
        lo[1] = pf(1, r0) * t + both
        lo[2] = pf(2, r0) * t + rsx[1]
        lo[3] = pf(3, r0) * t
        db[x] = lo[x]
        for d in (2, 1, 3):
            d_send(d).start()

    def finish_sources():
        for d in (1, 3, 2):
            d_in(d).wait_recv()

        loop(half, b1)
        loop(half, lambda i: b1_up_in(i).wait_recv())
        loop(heads, sources)

    def blocks_45():
        @pl.when(bits[3] == 1)
        def _():
            hand_on(0)

        @pl.when(bits[4] == 1)
        def _():
            hand_on(1)

    def chain_down():
        for j in range(2):
            b5_in(j).wait_recv()
        t = rz5[0] + rz5[1]
        za[0] = gp[0] + bf(3, r0) * t
        b4_send().start()
        dp[...] = t


    @pl.when(z == 7)
    def _():
        dp[...] = jnp.zeros((w, w), F32)

    loop(half, inside)
    @pl.when(bits[4] == 1)
    def _():
        bs_sum(1)

        @pl.when(z != 3)
        def _():
            za[1] = gp[1]
            b5_send().start()

    @pl.when(z % 2 == 1)
    def _():
        bs_sum(0)

        @pl.when(z == 7)
        def _():
            za[0] = gp[0]
            b4_send().start()


    @pl.when(core == 1)
    def _():
        loop(half, lambda i: f1_send(2 * i).wait_recv())

    @pl.when(z < 4)
    def _():
        @pl.when(z == 3)
        def _():
            for j in range(4):
                b6_in(j).wait_recv()
            t = rz6[0] + rz6[1] + rz6[2] + rz6[3]
            za[1] = gp[1] + bf(4, r0) * t
            b5_send().start()
            za[0] = gp[0] + bf(3, r0) * t
            b4_send().start()
            dp[...] = t

        blocks_45()
        x_blocks()
        loop(half, lambda i: inside(half + i))
        from_partner(range(1, 5))
        levels((0, 2), False)

        @pl.when(z == 1)
        def _():
            chain_down()

        levels((4,), True)
        level_sums()
        plane_gradient()
        finish_sources()

    @pl.when(z >= 4)
    def _():
        @pl.when(z == 5)
        def _():
            chain_down()

        z6_send(1).wait_recv()
        hand_round(2)
        loop(half, lambda i: inside(half + i))
        plane_gradient()
        x_blocks()
        blocks_45()
        from_partner(range(1, 5))
        levels((0, 2), False)
        hand_on(2)
        from_partner((5,))
        levels((4,), True)
        level_sums()
        finish_sources()

    for d in range(1, nh):
        h_send(d).wait_recv()
    tot = hb[0] + hb[1] + hb[2] + hb[3]
    glt[...] = tot[:LV_ALL, :]

    for j in range(3):
        loop(heads, lambda h: put(j, h).wait())
    for d in range(1, nh):
        h_send(d).wait_send()
    for j in range(7):
        g1(j).wait_send()
    for d in range(1, NZ):
        g3(d).wait_send()
    loop(half, lambda i: f1_send(other(i)).wait_send())

    @pl.when(core == 0)
    def _():
        loop(half, lambda i: f1_send(own(i)).wait_send())

    @pl.when(core == 1)
    def _():
        loop(half, lambda i: b1_early(i).wait_send())

    for d in range(1, NX):
        rs_send(d).wait_send()
        d_send(d).wait_send()

    for c in range(4):
        @pl.when(x != x_plan[c][0])
        def _():
            fx_send(c).wait_send()

        frm, l = b_plan[c]

        @pl.when(x == frm)
        def _():
            for d in range(1, NX):
                bx_send(c, l, d).wait_send()

    loop(half, lambda i: b1_up(i).wait_send())
    for l in range(1, LV):
        @pl.when(bits[l] == 1)
        def _():
            loop(half, lambda i: fwd(l, i).wait_send())
            loop(half, lambda i: gp_send(l, i).wait_send())

    for m in range(3):
        @pl.when(bits[3 + m] == 1)
        def _():
            for d in range(1, NX):
                bs_send(m, d).wait_send()
                ag_send(m, d).wait_send()

    @pl.when(z % 2 == 0)
    def _():
        z4_send().wait_send()

    @pl.when(z % 4 == 1)
    def _():
        z5_send(1).wait_send()
        z5_send(2).wait_send()

    @pl.when(z == 3)
    def _():
        for d in range(1, 5):
            z6_send(d).wait_send()

    @pl.when(z >= 4)
    def _():
        b6_send().wait_send()

    @pl.when(bits[4] == 1)
    def _():
        b5_send().wait_send()

    @pl.when(z % 2 == 1)
    def _():
        b4_send().wait_send()


def on_device(queries, key_input, value_input, grad_output, log_decay, level_weight, segment):
    n, heads = log_decay.shape
    width = queries.shape[1]
    w = 128
    half = heads // 2
    dma = pltpu.SemaphoreType.DMA

    def mem(*shape):
        return pltpu.VMEM(shape, F32)

    scratch = [mem(n, width) for _ in range(7)] + [mem(w, n)]
    scratch += [mem(heads, n, w), mem(heads, n, w), mem(heads, n, w), mem(LV_ALL, n, w),
                mem(w, n), mem(n, n), mem(LV, 8, w), mem(LV, 8, w), mem(LV, 8, w), mem(NX, 8, w), mem(LV_ALL, n, w)]
    scratch += [mem(8, 8, w), mem(NZ, 8, w), mem(heads, w, w), mem(LV, heads, w, w),
                mem(half, w, w), mem(w, w), mem(NX, w, w), mem(3, w, w),
                mem(LV, heads, w, w), mem(LV - 1, half, w, w), mem(3, half, w, w), mem(3, NX, w, w),
                mem(3, w, w), mem(2, w, w), mem(4, w, w), mem(2, w, w), mem(w, w), mem(NX, w, w)]
    scratch += [mem(2, half, w, w), mem(4, w, w), mem(NX, w, w), mem(w, w), mem(half, w, w)] + [mem(heads, w, w), mem(half, w, w), mem(4, 8, n),
                pltpu.VMEM((heads, w, 3 * n), BF16)]
    scratch += [dma((4,)), dma((3, heads))]
    for a, b in (((14,), (14,)), ((heads,), (heads,)), ((3,), (3,)), ((4,), (2, 3)), ((7,), (3,)),
                 ((3, 3), (3, 3)), ((LV - 1, half), (LV - 1, half)), ((LV - 1, half), (LV - 1, half)),
                 ((3, 3), (3, 3)), ((3,), (7,)), ((3,), (3,)), ((2, 3), (4,)),
                 ((heads,), (heads,)), ((3,), (3,))):
        scratch += [dma(a), dma(b)]
    vm = pl.BlockSpec(memory_space=pltpu.VMEM)
    hbm = pl.BlockSpec(memory_space=pl.ANY)
    out = jax.ShapeDtypeStruct((n, width), F32)
    dq, dk, dv, glt = pl.pallas_call(
        kernel,
        out_shape=(out, out, out, jax.ShapeDtypeStruct((LV_ALL, n), F32)),
        in_specs=[vm] * 3 + [hbm] * 4,
        out_specs=(hbm, hbm, hbm, vm),
        scratch_shapes=scratch,
        compiler_params=pltpu.CompilerParams(
            collective_id=0, has_side_effects=True, vmem_limit_bytes=60 << 20),
    )(log_decay.T, level_weight.T, segment[None, :], queries, key_input, value_input, grad_output)
    return dq, dk, dv, glt.T


def solution(mesh):
    in_specs = (
        P("seq", "head"),
        P("seq", "head"),
        P("seq", "head"),
        P("seq", "head"),
        P("seq", "head"),
        P("seq", None),
        P("seq"),
    )
    out_specs = (P("seq", "head"), P("seq", "head"), P("seq", "head"), P("seq", None))
    return jax.shard_map(
        on_device, mesh=mesh, in_specs=in_specs, out_specs=out_specs, check_vma=False
    )
```

time: 77.7 us -> 64.4 us (0.83)
  the two profiles are of different devices: /device:TPU:8 before, /device:TPU:105 now
where the time goes in v1:
time: 64.4 us; the launch traced here: 64.2 us
  Pallas kernels  58 us (90%)
  local copies, waits for them, and re-layouts  5.57 us (9%)
  between operations  0.65 us (1%)
    pallas_call x1, Pallas kernels, on_device(): pl.pallas_call(kernel, out_shape=(out, out, out, jax.ShapeDtypeStruct((LV...  58 us
    unnamed x10, local copies, waits for them, and re-layouts  5.57 us

profile of v1, /device:TPU:105, one launch (start us, length us, event | category | flops | bytes accessed | tf_op | source)
XLA Modules:
  0.0 64.2 jit_solution(4749310330557568688)
XLA Ops:
  0.6 58.0 %shard_map.102 = (f32[256,1024]{1,0:T(8,128)}, f32[256,1024]{1,0:T(8,128)}, f32[256,1024]{1,0:T(8,128)}, f32[7,256]{1,0:T(8,128)}) custom-call(f32[8,256]{1,0:T(8,128)} %bitcast.4, f32[7,256]{1,0:T(8,128)} %bitcast.5, s32[1,256]{1,0:T(1,128)} %bitcast.7, f32[256,1024]{1,0:T(8,128)} %q_hbm.1, f32[256,1024]{1,0:T(8,128)} %k_hbm.1, f32[256,1024]{1,0:T(8,128)} %v_hbm.1, ...), custom_call_target="tpu_custom_call" | custom-call | tf_op jit(solution)/shard_map/pallas_call | solution.py:827
  58.6 0.0 copy-start.1
  58.6 2.4 %copy.15 = f32[256,1024]{1,0:T(8,128)} copy(f32[256,1024]{1,0:T(8,128)} %get-tuple-element.16) | data formatting | bytes 2097152
  61.0 0.0 copy-done.1
  61.0 0.0 copy-start
  61.0 1.0 %copy.16 = f32[256,1024]{1,0:T(8,128)} copy(f32[256,1024]{1,0:T(8,128)S(1)} %copy-done.1) | data formatting | bytes 2097152
  62.0 0.6 copy-done
  62.6 0.0 copy-start.2
  62.6 1.0 %copy.17 = f32[256,1024]{1,0:T(8,128)} copy(f32[256,1024]{1,0:T(8,128)S(1)} %copy-done) | data formatting | bytes 2097152
  63.6 0.0 copy-done.2
  63.6 0.6 copy.18
Async XLA Ops:
  58.6 2.4 %copy-start.1 = (f32[256,1024]{1,0:T(8,128)S(1)}, f32[256,1024]{1,0:T(8,128)}, u32[]{:S(2)}) copy-start(f32[256,1024]{1,0:T(8,128)} %get-tuple-element.17) | copy-start | bytes 3145732
  61.0 1.6 %copy-start = (f32[256,1024]{1,0:T(8,128)S(1)}, f32[256,1024]{1,0:T(8,128)}, u32[]{:S(2)}) copy-start(f32[256,1024]{1,0:T(8,128)} %get-tuple-element.18) | copy-start | bytes 3145732
  62.6 1.0 %copy-start.2 = (f32[7,256]{1,0:T(8,128)S(1)}, f32[7,256]{1,0:T(8,128)}, u32[]{:S(2)}) copy-start(f32[7,256]{1,0:T(8,128)} %get-tuple-element.11) | copy-start | bytes 21508

commit v2 on v1

--- a/solution.py
+++ b/solution.py
@@ -39,12 +39,12 @@
     lax.fori_loop(0, n, body, 0)
 
 
-def kernel(ldt, lwt, sgt, q_hbm, k_hbm, v_hbm, o_hbm, dq_hbm, dk_hbm, dv_hbm, glt,
-           q, k, v, o, dq, dk, dv, packt,
+def kernel(ldt, lwt, sgt, q_hbm, k_hbm, v_hbm, o_hbm, dq, dk, dv, glt,
+           q, k, v, o, packt,
            cumcol, ecol, swcol, lwcol, cumt, bias, bfac, gfac, hfac, pfac, lev,
            pb, zt, st, rf, tt, t01, rsb, zs, gs, gr, gx, rsg, gp, za, rz6, rz5, rz4, db,
            gxx, rsx, lo, dp, ge, rl, ml, hb, olhs,
-           s_in, s_out, s_g, r_g, s_1, r_1, s_rs, r_rs, s_x, r_x, s_z, r_z, s_ag, r_ag, s_f, r_f, s_p, r_p,
+           s_in, s_g, r_g, s_1, r_1, s_rs, r_rs, s_x, r_x, s_z, r_z, s_ag, r_ag, s_f, r_f, s_p, r_p,
            s_bs, r_bs, s_bz, r_bz, s_d, r_d, s_m, r_m, s_b1, r_b1, s_h, r_h):
     n, heads, w = q.shape[0], swcol.shape[0], 128
     half = heads // 2
@@ -82,6 +82,7 @@
 
     peers = [plane_dev(d, e) for d, e in plane_peers]
     peers += [at((z + d) % NZ, x, core) for d in range(1, NZ)]
+    peers += [at((z + e) % NZ, (x + d) % NX, core) for d in range(1, NX) for e in (1, NZ - 1)]
     peers += [(me, (hd + d) % nh) for d in range(1, nh)]
     for dev in peers:
         pl.semaphore_signal(barrier, inc=1, device_id=dev, device_id_type=pl.DeviceIdType.MESH)
@@ -107,17 +108,6 @@
     own_row = jnp.where(lane1 == heads + 1, jnp.broadcast_to(pk[0:1, 15:16], (1, w)), own_row)
     pb[r0] = jnp.broadcast_to(own_row, (8, w))
 
-    pl.semaphore_wait(barrier, len(peers))
-
-    def g1(j):
-        d, e = plane_peers[j]
-        return cp(pb.at[r0], pb.at[r0], s_g.at[j], r_g.at[j], plane_dev(d, e))
-
-    def g3(d):
-        return cp(zt.at[z], zt.at[z], s_g.at[6 + d], r_g.at[6 + d], at((z + d) % NZ, x, core))
-
-    for j in range(7):
-        g1(j).start()
     sw = jnp.exp(total - cum) * (seg == own_end).astype(F32)
     for h in range(heads):
         swcol[h] = jnp.broadcast_to(sw[:, h:h + 1], (n, w))
@@ -143,7 +133,6 @@
 
     def state_other(i):
         make_state(other(i))
-        f1_send(other(i)).start()
 
     def state_own(i):
         make_state(own(i))
@@ -152,8 +141,6 @@
         def _():
             f1_send(own(i)).start()
 
-    loop(half, state_other)
-    loop(half, state_own)
     first = pk[0:1, 15:16]
     ecum = jnp.exp(cum) * (seg == first).astype(F32)
     for h in range(heads):
@@ -161,6 +148,20 @@
     for l in range(LV_ALL):
         lwcol[l] = jnp.broadcast_to(pk[:, 8 + l:9 + l], (n, w))
 
+
+    loop(half, state_other)
+    pl.semaphore_wait(barrier, len(peers))
+    def g1(j):
+        d, e = plane_peers[j]
+        return cp(pb.at[r0], pb.at[r0], s_g.at[j], r_g.at[j], plane_dev(d, e))
+
+    def g3(d):
+        return cp(zt.at[z], zt.at[z], s_g.at[6 + d], r_g.at[6 + d], at((z + d) % NZ, x, core))
+
+    for j in range(7):
+        g1(j).start()
+    loop(half, lambda i: f1_send(other(i)).start())
+    loop(half, state_own)
     def gp_send(l, i):
         return cp(gs.at[l, other(i)], gr.at[l - 1, i], s_p.at[l - 1, i], r_p.at[l - 1, i], partner)
 
@@ -194,6 +195,7 @@
     bring(2).wait()
     bring(3).wait()
     loop(half, g_other(4))
+    loop(half, g_own(4))
     for j in range(7):
         g1(j).wait_recv()
     sub = lax.broadcasted_iota(jnp.int32, (8, w), 0)
@@ -257,7 +259,6 @@
     for d in (2, 1, 3):
         rs_send(d).start()
 
-    loop(half, g_own(4))
     loop(half, g_other(2))
     for h in range(heads):
         cumcol[h] = jnp.broadcast_to(cum[:, h:h + 1], (n, w))
@@ -269,6 +270,8 @@
         lev[l] = jnp.zeros((n, w), F32)
 
     loop(half, g_own(2))
+    loop(half, g_other(0))
+    loop(half, g_own(0))
 
     for d in (1, 3, 2):
         rs_in(d).wait_recv()
@@ -287,9 +290,14 @@
     def z6_send(d):
         return cp(zs.at[2], rf.at[5, r0], s_z.at[2 + d], r_z.at[2], at((z + d) % NZ, x, core))
 
+    def z4_round(d):
+        return cp(zs.at[0], rf.at[3, r0], s_ag.at[0, d - 1], r_ag.at[0, d - 1], at((z + 1) % NZ, (x + d) % NX, core))
+
     @pl.when(z % 2 == 0)
     def _():
         z4_send().start()
+        for d in (2, 1, 3):
+            z4_round(d).start()
 
     for d in range(1, NZ):
         g3(d).wait_recv()
@@ -313,11 +321,13 @@
 
     def bs_send(m, d):
         i = (x + d) % NX
-        return cp(gx.at[m, i], rsg.at[m, x], s_bs.at[m, d - 1], r_bs.at[m, d - 1], at(z, i, core))
+        to = z if m else (z + NZ - 1) % NZ
+        return cp(gx.at[m, i], rsg.at[m, x], s_bs.at[m, (d + 3) % 4], r_bs.at[m, (d + 3) % 4], at(to, i, core))
 
     def bs_in(m, d):
         j = (x + NX - d) % NX
-        return cp(gx.at[m, x], rsg.at[m, j], s_bs.at[m, d - 1], r_bs.at[m, d - 1], at(z, j, core))
+        frm = z if m else (z + 1) % NZ
+        return cp(gx.at[m, x], rsg.at[m, j], s_bs.at[m, (d + 3) % 4], r_bs.at[m, (d + 3) % 4], at(frm, j, core))
 
     def bs_out(m):
         @pl.when(bits[3 + m] == 1)
@@ -327,7 +337,7 @@
                 gx[m, i] = gsum(3 + m, i)
 
             loop(half, one)
-            for d in (2, 1, 3):
+            for d in (2, 1, 3) if m else (2, 1, 3, 0):
                 bs_send(m, d).start()
 
     def bs_sum(m):
@@ -337,143 +347,6 @@
         for d in range(1, NX):
             t = t + rsg[m, (x + NX - d) % NX]
         gp[m] = t
-
-    bs_out(2)
-    bs_out(1)
-    bs_out(0)
-    loop(half, g_other(0))
-    loop(half, g_own(0))
-
-    def ag_send(m, d):
-        slot = rf.at[3 + m, r0]
-        return cp(slot, slot, s_ag.at[m, d - 1], r_ag.at[m, d - 1], at(z, (x + d) % NX, core))
-
-    def ag_in(m, d):
-        slot = rf.at[3 + m, own((x + NX - d) % NX)]
-        return cp(slot, slot, s_ag.at[m, d - 1], r_ag.at[m, d - 1], at(z, (x + NX - d) % NX, core))
-
-    def fwd(l, i):
-        slot = rf.at[l, own(i)]
-        return cp(slot, slot, s_f.at[l - 1, i], r_f.at[l - 1, i], partner)
-
-    def fwd_in(l, i):
-        slot = rf.at[l, other(i)]
-        return cp(slot, slot, s_f.at[l - 1, i], r_f.at[l - 1, i], partner)
-
-    def hand_round(m):
-        for d in (2, 1, 3):
-            ag_send(m, d).start()
-        fwd(3 + m, x).start()
-
-    def hand_on(m):
-        for d in (1, 3, 2):
-            ag_in(m, d).wait_recv()
-            fwd(3 + m, (x + NX - d) % NX).start()
-
-    @pl.when(z % 2 == 1)
-    def _():
-        z4_send().wait_recv()
-        zs[1] = bf(3, r0) * rf[3, r0] + zs[0]
-
-        @pl.when((z // 2) % 2 == 0)
-        def _():
-            z5_send(2).start()
-            z5_send(1).start()
-
-    @pl.when(z % 2 == 1)
-    def _():
-        hand_round(0)
-
-    def bx_send(c, l, d):
-        i = (x + d) % NX
-        return cp(gxx.at[l - 1, i], rsx.at[c], s_m.at[l - 1, d - 1], r_m.at[c], at(z, i, core))
-
-    def bx_in(c, l):
-        return cp(gxx.at[l - 1, x], rsx.at[c], s_m.at[l - 1, 0], r_m.at[c], at(z, x, 1 - core))
-
-    b_plan = ((1, 1), (3, 1), (2, 2), (3, 2))
-    for c in (2, 3, 0, 1):
-        frm, l = b_plan[c]
-
-        @pl.when(x == frm)
-        def _():
-            def one(i):
-                gp_send(l, i).wait_recv()
-                gxx[l - 1, i] = gsum(l, i)
-
-            loop(half, one)
-            rsx[c] = gxx[l - 1, x]
-            for d in (2, 1, 3):
-                bx_send(c, l, d).start()
-
-    t01[...] = bf(1, r0) * rsb[0] + rsb[1]
-    x_plan = ((1, 1, 0), (3, 1, 2), (2, 2, None), (3, 2, None))
-
-    def fx_send(c):
-        to, l, j = x_plan[c]
-        src = t01 if j is None else rsb.at[j]
-        return cp(src, rf.at[l, r0], s_x.at[c], r_x.at[l - 1, (to + NX - x + 3) % NX], at(z, to, core))
-
-    def fx_in(l, d):
-        j = (x + NX - d) % NX
-        return cp(t01, rf.at[l, own(j)], s_x.at[0], r_x.at[l - 1, d - 1], at(z, j, core))
-
-    for c in range(4):
-        to, l, j = x_plan[c]
-
-        @pl.when(x == to)
-        def _():
-            rf[l, r0] = t01[...] if j is None else rsb[j]
-
-        @pl.when(x != to)
-        def _():
-            fx_send(c).start()
-
-    def b6_send():
-        return cp(gp.at[2], rz6.at[z % 4], s_bz.at[0], r_bz.at[z % 4], at(3, x, core))
-
-    def b6_in(j):
-        return cp(gp.at[2], rz6.at[j], s_bz.at[0], r_bz.at[j], at(4 + j, x, core))
-
-    def b5_send():
-        return cp(za.at[1], rz5.at[z % 2], s_bz.at[1], r_bz.at[4 + z % 2], at(4 * (z // 4) + 1, x, core))
-
-    def b5_in(j):
-        return cp(za.at[1], rz5.at[j], s_bz.at[1], r_bz.at[4 + j], at((z + 1 + j) % NZ, x, core))
-
-    def b4_send():
-        return cp(za.at[0], rz4, s_bz.at[2], r_bz.at[6], at((z + NZ - 1) % NZ, x, core))
-
-    @pl.when(z >= 4)
-    def _():
-        bs_sum(2)
-        b6_send().start()
-
-    @pl.when(z == 3)
-    def _():
-        z5_send(1).wait_recv()
-        zs[2] = bf(4, r0) * rf[4, r0] + zs[1]
-        for d in (4, 3, 2, 1):
-            z6_send(d).start()
-
-    @pl.when(bits[4] == 1)
-    def _():
-        @pl.when(z != 3)
-        def _():
-            z5_send(1).wait_recv()
-
-        hand_round(1)
-
-    def b1_early(i):
-        return cp(ge.at[i], rl.at[2 * i], s_b1.at[i], r_b1.at[i], partner)
-
-    @pl.when(core == 1)
-    def _():
-        def one(i):
-            ge[i] = gs[0, 2 * i] * gf(0, 2 * i)
-            b1_early(i).start()
-
-        loop(half, one)
 
     def inside(h):
         hc = head_cols(h)
@@ -493,6 +366,144 @@
         dv[:, hc] = mm(left(a.T, 1), right(oh, 0), 1, 0)
         dk[:, hc] = mm(left(b.T, 1), right(qh, 0), 1, 0)
 
+    bs_out(2)
+    bs_out(1)
+    bs_out(0)
+    loop(2, inside)
+
+    def ag_send(m, d):
+        slot = rf.at[3 + m, r0]
+        return cp(slot, slot, s_ag.at[m, d - 1], r_ag.at[m, d - 1], at(z, (x + d) % NX, core))
+
+    def ag_in(m, d):
+        slot = rf.at[3 + m, own((x + NX - d) % NX)]
+        return cp(slot, slot, s_ag.at[m, d - 1], r_ag.at[m, d - 1], at(z, (x + NX - d) % NX, core))
+
+    def fwd(l, i):
+        slot = rf.at[l, own(i)]
+        return cp(slot, slot, s_f.at[l - 1, i], r_f.at[l - 1, i], partner)
+
+    def fwd_in(l, i):
+        slot = rf.at[l, other(i)]
+        return cp(slot, slot, s_f.at[l - 1, i], r_f.at[l - 1, i], partner)
+
+    def hand_round(m):
+        for d in (2, 1, 3):
+            ag_send(m, d).start()
+        fwd(3 + m, x).start()
+
+    def hand_on(m):
+        for d in (1, 3, 2):
+            ag_in(m, d).wait_recv()
+            fwd(3 + m, (x + NX - d) % NX).start()
+
+    @pl.when(z % 2 == 1)
+    def _():
+        z4_send().wait_recv()
+        zs[1] = bf(3, r0) * rf[3, r0] + zs[0]
+
+        @pl.when((z // 2) % 2 == 0)
+        def _():
+            z5_send(2).start()
+            z5_send(1).start()
+
+    @pl.when(z % 2 == 1)
+    def _():
+        fwd(3, x).start()
+
+    def bx_send(c, l, d):
+        i = (x + d) % NX
+        return cp(gxx.at[l - 1, i], rsx.at[c], s_m.at[l - 1, d - 1], r_m.at[c], at(z, i, core))
+
+    def bx_in(c, l):
+        return cp(gxx.at[l - 1, x], rsx.at[c], s_m.at[l - 1, 0], r_m.at[c], at(z, x, 1 - core))
+
+    b_plan = ((1, 1), (3, 1), (2, 2), (3, 2))
+    for c in (2, 3, 0, 1):
+        frm, l = b_plan[c]
+
+        @pl.when(x == frm)
+        def _():
+            def one(i):
+                gp_send(l, i).wait_recv()
+                gxx[l - 1, i] = gsum(l, i)
+
+            loop(half, one)
+            rsx[c] = gxx[l - 1, x]
+            for d in (2, 1, 3):
+                bx_send(c, l, d).start()
+
+    t01[...] = bf(1, r0) * rsb[0] + rsb[1]
+    x_plan = ((1, 1, 0), (3, 1, 2), (2, 2, None), (3, 2, None))
+
+    def fx_send(c):
+        to, l, j = x_plan[c]
+        src = t01 if j is None else rsb.at[j]
+        return cp(src, rf.at[l, r0], s_x.at[c], r_x.at[l - 1, (to + NX - x + 3) % NX], at(z, to, core))
+
+    def fx_in(l, d):
+        j = (x + NX - d) % NX
+        return cp(t01, rf.at[l, own(j)], s_x.at[0], r_x.at[l - 1, d - 1], at(z, j, core))
+
+    for c in range(4):
+        to, l, j = x_plan[c]
+
+        @pl.when(x == to)
+        def _():
+            rf[l, r0] = t01[...] if j is None else rsb[j]
+
+        @pl.when(x != to)
+        def _():
+            fx_send(c).start()
+
+    def b6_send():
+        return cp(gp.at[2], rz6.at[z % 4], s_bz.at[0], r_bz.at[z % 4], at(3, x, core))
+
+    def b6_in(j):
+        return cp(gp.at[2], rz6.at[j], s_bz.at[0], r_bz.at[j], at(4 + j, x, core))
+
+    def b5_send():
+        return cp(za.at[1], rz5.at[z % 2], s_bz.at[1], r_bz.at[4 + z % 2], at(4 * (z // 4) + 1, x, core))
+
+    def b5_in(j):
+        return cp(za.at[1], rz5.at[j], s_bz.at[1], r_bz.at[4 + j], at((z + 1 + j) % NZ, x, core))
+
+    def b4_send():
+        return cp(za.at[0], rz4, s_bz.at[2], r_bz.at[6], at((z + NZ - 1) % NZ, x, core))
+
+    @pl.when(z >= 4)
+    def _():
+        bs_sum(2)
+        b6_send().start()
+
+    loop(2, lambda i: inside(2 + i))
+
+    @pl.when(z == 3)
+    def _():
+        z5_send(1).wait_recv()
+        zs[2] = bf(4, r0) * rf[4, r0] + zs[1]
+        for d in (4, 3, 2, 1):
+            z6_send(d).start()
+
+    @pl.when(bits[4] == 1)
+    def _():
+        @pl.when(z != 3)
+        def _():
+            z5_send(1).wait_recv()
+
+        hand_round(1)
+
+    def b1_early(i):
+        return cp(ge.at[i], rl.at[2 * i], s_b1.at[i], r_b1.at[i], partner)
+
+    @pl.when(core == 1)
+    def _():
+        def one(i):
+            ge[i] = gs[0, 2 * i] * gf(0, 2 * i)
+            b1_early(i).start()
+
+        loop(half, one)
+
     def d_send(d):
         return cp(lo.at[(x + d) % NX], db.at[x], s_d.at[d - 1], r_d.at[d - 1], at(z, (x + d) % NX, core))
 
@@ -522,12 +533,7 @@
 
         b1_up(i).start()
 
-    def put(j, h):
-        src, dst = ((dq, dq_hbm), (dk, dk_hbm), (dv, dv_hbm))[j]
-        hc = head_cols(h)
-        return pltpu.make_async_copy(src.at[:, hc], dst.at[:, hc], s_out.at[j, h])
-
-    def levels(pairs, last):
+    def levels(pairs):
         def one(h):
             hc = head_cols(h)
             oh = left(o[:, hc], 1)
@@ -544,8 +550,6 @@
                     lev[m + 1] += qh * part
                     acc = acc + lwcol[m + 1] * part
             dq[:, hc] = acc
-            if last:
-                put(0, h).start()
 
         loop(heads, one)
 
@@ -554,9 +558,7 @@
         g = rl[h]
         s = swcol[h]
         dk[:, hc] += s * mm(left(v[:, hc], 1), right(g, 0), 1, 0)
-        put(1, h).start()
         dv[:, hc] += s * mm(left(k[:, hc], 1), right(g, 1), 1, 1)
-        put(2, h).start()
 
     def h_send(d):
         return cp(hb.at[hd], hb.at[hd], s_h.at[d - 1], r_h.at[d - 1], (me, (hd + d) % nh))
@@ -594,8 +596,14 @@
     def plane_gradient():
         @pl.when(z % 2 == 0)
         def _():
-            b4_send().wait_recv()
-            dp[...] = rz4[...]
+            for d in (0, 1, 3, 2):
+                bs_in(0, d).wait_recv()
+            dp[...] = rsg[0, 0] + rsg[0, 1] + rsg[0, 2] + rsg[0, 3]
+
+            @pl.when(z != 6)
+            def _():
+                b4_send().wait_recv()
+                dp[...] += rz4[...]
 
         for c in range(4):
             frm, l = b_plan[c]
@@ -635,16 +643,89 @@
         for j in range(2):
             b5_in(j).wait_recv()
         t = rz5[0] + rz5[1]
-        za[0] = gp[0] + bf(3, r0) * t
+        za[0] = bf(3, r0) * t
         b4_send().start()
         dp[...] = t
 
 
+    def drain():
+        for j in range(7):
+            g1(j).wait_send()
+        for d in range(1, NZ):
+            g3(d).wait_send()
+        loop(half, lambda i: f1_send(other(i)).wait_send())
+
+        @pl.when(core == 0)
+        def _():
+            loop(half, lambda i: f1_send(own(i)).wait_send())
+
+        @pl.when(core == 1)
+        def _():
+            loop(half, lambda i: b1_early(i).wait_send())
+
+        for d in range(1, NX):
+            rs_send(d).wait_send()
+
+        for c in range(4):
+            @pl.when(x != x_plan[c][0])
+            def _():
+                fx_send(c).wait_send()
+
+            frm, l = b_plan[c]
+
+            @pl.when(x == frm)
+            def _():
+                for d in range(1, NX):
+                    bx_send(c, l, d).wait_send()
+
+        for l in range(1, LV):
+            @pl.when(bits[l] == 1)
+            def _():
+                loop(half, lambda i: fwd(l, i).wait_send())
+                loop(half, lambda i: gp_send(l, i).wait_send())
+
+        for m in range(3):
+            @pl.when(bits[3 + m] == 1)
+            def _():
+                for d in range(1 if m else 0, NX):
+                    bs_send(m, d).wait_send()
+                if m:
+                    for d in range(1, NX):
+                        ag_send(m, d).wait_send()
+
+        @pl.when(z % 2 == 0)
+        def _():
+            z4_send().wait_send()
+            for d in range(1, NX):
+                z4_round(d).wait_send()
+
+        @pl.when(z % 4 == 1)
+        def _():
+            z5_send(1).wait_send()
+            z5_send(2).wait_send()
+
+        @pl.when(z == 3)
+        def _():
+            for d in range(1, 5):
+                z6_send(d).wait_send()
+
+        @pl.when(z >= 4)
+        def _():
+            b6_send().wait_send()
+
+        @pl.when(bits[4] == 1)
+        def _():
+            b5_send().wait_send()
+
+        @pl.when((z % 2 == 1) & (z != 7))
+        def _():
+            b4_send().wait_send()
+
     @pl.when(z == 7)
     def _():
         dp[...] = jnp.zeros((w, w), F32)
 
-    loop(half, inside)
+    loop(2, lambda i: inside(4 + i))
     @pl.when(bits[4] == 1)
     def _():
         bs_sum(1)
@@ -653,16 +734,6 @@
         def _():
             za[1] = gp[1]
             b5_send().start()
-
-    @pl.when(z % 2 == 1)
-    def _():
-        bs_sum(0)
-
-        @pl.when(z == 7)
-        def _():
-            za[0] = gp[0]
-            b4_send().start()
-
 
     @pl.when(core == 1)
     def _():
@@ -677,23 +748,32 @@
             t = rz6[0] + rz6[1] + rz6[2] + rz6[3]
             za[1] = gp[1] + bf(4, r0) * t
             b5_send().start()
-            za[0] = gp[0] + bf(3, r0) * t
+            za[0] = bf(3, r0) * t
             b4_send().start()
             dp[...] = t
 
+        loop(2, lambda i: inside(6 + i))
+
+        @pl.when(z == 1)
+        def _():
+            chain_down()
+
+        @pl.when(z != 0)
+        def _():
+            plane_gradient()
+
         blocks_45()
         x_blocks()
-        loop(half, lambda i: inside(half + i))
         from_partner(range(1, 5))
-        levels((0, 2), False)
-
-        @pl.when(z == 1)
-        def _():
-            chain_down()
-
-        levels((4,), True)
+        levels((0, 2))
+        levels((4,))
         level_sums()
-        plane_gradient()
+        drain()
+
+        @pl.when(z == 0)
+        def _():
+            plane_gradient()
+
         finish_sources()
 
     @pl.when(z >= 4)
@@ -704,96 +784,29 @@
 
         z6_send(1).wait_recv()
         hand_round(2)
-        loop(half, lambda i: inside(half + i))
+        loop(2, lambda i: inside(6 + i))
         plane_gradient()
         x_blocks()
         blocks_45()
         from_partner(range(1, 5))
-        levels((0, 2), False)
+        levels((0, 2))
         hand_on(2)
         from_partner((5,))
-        levels((4,), True)
+        levels((4,))
         level_sums()
         finish_sources()
+        drain()
 
     for d in range(1, nh):
         h_send(d).wait_recv()
     tot = hb[0] + hb[1] + hb[2] + hb[3]
     glt[...] = tot[:LV_ALL, :]
 
-    for j in range(3):
-        loop(heads, lambda h: put(j, h).wait())
     for d in range(1, nh):
         h_send(d).wait_send()
-    for j in range(7):
-        g1(j).wait_send()
-    for d in range(1, NZ):
-        g3(d).wait_send()
-    loop(half, lambda i: f1_send(other(i)).wait_send())
-
-    @pl.when(core == 0)
-    def _():
-        loop(half, lambda i: f1_send(own(i)).wait_send())
-
-    @pl.when(core == 1)
-    def _():
-        loop(half, lambda i: b1_early(i).wait_send())
-
     for d in range(1, NX):
-        rs_send(d).wait_send()
         d_send(d).wait_send()
-
-    for c in range(4):
-        @pl.when(x != x_plan[c][0])
-        def _():
-            fx_send(c).wait_send()
-
-        frm, l = b_plan[c]
-
-        @pl.when(x == frm)
-        def _():
-            for d in range(1, NX):
-                bx_send(c, l, d).wait_send()
-
     loop(half, lambda i: b1_up(i).wait_send())
-    for l in range(1, LV):
-        @pl.when(bits[l] == 1)
-        def _():
-            loop(half, lambda i: fwd(l, i).wait_send())
-            loop(half, lambda i: gp_send(l, i).wait_send())
-
-    for m in range(3):
-        @pl.when(bits[3 + m] == 1)
-        def _():
-            for d in range(1, NX):
-                bs_send(m, d).wait_send()
-                ag_send(m, d).wait_send()
-
-    @pl.when(z % 2 == 0)
-    def _():
-        z4_send().wait_send()
-
-    @pl.when(z % 4 == 1)
-    def _():
-        z5_send(1).wait_send()
-        z5_send(2).wait_send()
-
-    @pl.when(z == 3)
-    def _():
-        for d in range(1, 5):
-            z6_send(d).wait_send()
-
-    @pl.when(z >= 4)
-    def _():
-        b6_send().wait_send()
-
-    @pl.when(bits[4] == 1)
-    def _():
-        b5_send().wait_send()
-
-    @pl.when(z % 2 == 1)
-    def _():
-        b4_send().wait_send()
 
 
 def on_device(queries, key_input, value_input, grad_output, log_decay, level_weight, segment):
@@ -806,7 +819,7 @@
     def mem(*shape):
         return pltpu.VMEM(shape, F32)
 
-    scratch = [mem(n, width) for _ in range(7)] + [mem(w, n)]
+    scratch = [mem(n, width) for _ in range(4)] + [mem(w, n)]
     scratch += [mem(heads, n, w), mem(heads, n, w), mem(heads, n, w), mem(LV_ALL, n, w),
                 mem(w, n), mem(n, n), mem(LV, 8, w), mem(LV, 8, w), mem(LV, 8, w), mem(NX, 8, w), mem(LV_ALL, n, w)]
     scratch += [mem(8, 8, w), mem(NZ, 8, w), mem(heads, w, w), mem(LV, heads, w, w),
@@ -815,20 +828,20 @@
                 mem(3, w, w), mem(2, w, w), mem(4, w, w), mem(2, w, w), mem(w, w), mem(NX, w, w)]
     scratch += [mem(2, half, w, w), mem(4, w, w), mem(NX, w, w), mem(w, w), mem(half, w, w)] + [mem(heads, w, w), mem(half, w, w), mem(4, 8, n),
                 pltpu.VMEM((heads, w, 3 * n), BF16)]
-    scratch += [dma((4,)), dma((3, heads))]
+    scratch += [dma((4,))]
     for a, b in (((14,), (14,)), ((heads,), (heads,)), ((3,), (3,)), ((4,), (2, 3)), ((7,), (3,)),
                  ((3, 3), (3, 3)), ((LV - 1, half), (LV - 1, half)), ((LV - 1, half), (LV - 1, half)),
-                 ((3, 3), (3, 3)), ((3,), (7,)), ((3,), (3,)), ((2, 3), (4,)),
+                 ((3, 4), (3, 4)), ((3,), (7,)), ((3,), (3,)), ((2, 3), (4,)),
                  ((heads,), (heads,)), ((3,), (3,))):
         scratch += [dma(a), dma(b)]
     vm = pl.BlockSpec(memory_space=pltpu.VMEM)
     hbm = pl.BlockSpec(memory_space=pl.ANY)
-    out = jax.ShapeDtypeStruct((n, width), F32)
+    out = pltpu.VMEM((n, width), F32)
     dq, dk, dv, glt = pl.pallas_call(
         kernel,
-        out_shape=(out, out, out, jax.ShapeDtypeStruct((LV_ALL, n), F32)),
+        out_shape=(out, out, out, pltpu.VMEM((LV_ALL, n), F32)),
         in_specs=[vm] * 3 + [hbm] * 4,
-        out_specs=(hbm, hbm, hbm, vm),
+        out_specs=(vm,) * 4,
         scratch_shapes=scratch,
         compiler_params=pltpu.CompilerParams(
             collective_id=0, has_side_effects=True, vmem_limit_bytes=60 << 20),

time: 64.4 us -> 57.2 us (0.89)
  the two profiles are of different devices: /device:TPU:105 before, /device:TPU:1 now
where the time goes in v2:
time: 57.2 us; the launch traced here: 57.1 us
  Pallas kernels  53 us (93%)
  local copies, waits for them, and re-layouts  3.51 us (6%)
  between operations  0.64 us (1%)
    pallas_call x1, Pallas kernels, on_device(): pl.pallas_call(kernel, out_shape=(out, out, out, pltpu.VMEM((LV_ALL, n),...  53 us
    unnamed x4, local copies, waits for them, and re-layouts  3.51 us

profile of v2, /device:TPU:1, one launch (start us, length us, event | category | flops | bytes accessed | tf_op | source)
XLA Modules:
  0.0 57.1 jit_solution(931092881335571487)
XLA Ops:
  0.6 53.0 %shard_map.102 = (f32[256,1024]{1,0:T(8,128)S(1)}, f32[256,1024]{1,0:T(8,128)S(1)}, f32[256,1024]{1,0:T(8,128)S(1)}, f32[7,256]{1,0:T(8,128)S(1)}) custom-call(f32[8,256]{1,0:T(8,128)} %bitcast.5, f32[7,256]{1,0:T(8,128)} %bitcast.6, s32[1,256]{1,0:T(1,128)} %bitcast.7, f32[256,1024]{1,0:T(8,128)} %q_hbm.1, f32[256,1024]{1,0:T(8,128)} %k_hbm.1, ...), custom_call_target="tpu_custom_call" | custom-call | tf_op jit(solution)/shard_map/pallas_call | solution.py:840
  53.6 1.0 %copy.15 = f32[256,1024]{1,0:T(8,128)} copy(f32[256,1024]{1,0:T(8,128)S(1)} %get-tuple-element.12) | data formatting | bytes 2097152
  54.6 0.6 %copy.18 = f32[256,7]{0,1:T(8,128)} copy(f32[256,7]{0,1:T(8,128)S(1)} %bitcast.4) | data formatting | bytes 14336
  55.2 1.0 %copy.16 = f32[256,1024]{1,0:T(8,128)} copy(f32[256,1024]{1,0:T(8,128)S(1)} %get-tuple-element.13) | data formatting | bytes 2097152
  56.1 1.0 %copy.17 = f32[256,1024]{1,0:T(8,128)} copy(f32[256,1024]{1,0:T(8,128)S(1)} %get-tuple-element.14) | data formatting | bytes 2097152

commit v3 on v2

--- a/solution.py
+++ b/solution.py
@@ -149,7 +149,10 @@
         lwcol[l] = jnp.broadcast_to(pk[:, 8 + l:9 + l], (n, w))
 
 
-    loop(half, state_other)
+    @pl.when(z < 4)
+    def _():
+        loop(half, state_other)
+
     pl.semaphore_wait(barrier, len(peers))
     def g1(j):
         d, e = plane_peers[j]
@@ -160,6 +163,11 @@
 
     for j in range(7):
         g1(j).start()
+
+    @pl.when(z >= 4)
+    def _():
+        loop(half, state_other)
+
     loop(half, lambda i: f1_send(other(i)).start())
     loop(half, state_own)
     def gp_send(l, i):
@@ -627,8 +635,9 @@
             d_in(d).wait_recv()
 
         loop(half, b1)
+        loop(half, lambda i: sources(own(i)))
         loop(half, lambda i: b1_up_in(i).wait_recv())
-        loop(heads, sources)
+        loop(half, lambda i: sources(other(i)))
 
     def blocks_45():
         @pl.when(bits[3] == 1)
@@ -789,8 +798,8 @@
         x_blocks()
         blocks_45()
         from_partner(range(1, 5))
+        hand_on(2)
         levels((0, 2))
-        hand_on(2)
         from_partner((5,))
         levels((4,))
         level_sums()

time: 57.2 us -> 56.1 us (0.981)
  Pallas kernels: 53 us -> 51.8 us
    pallas_call x1, Pallas kernels: 53 us -> 51.8 us  [on_device(): pl.pallas_call(kernel, out_shape=(out, out, out, pltpu.VMEM((LV_ALL, n),...]
where the time goes in v3:
time: 56.1 us; the launch traced here: 56 us
  Pallas kernels  51.8 us (92%)
  local copies, waits for them, and re-layouts  3.51 us (6%)
  between operations  0.64 us (1%)
    pallas_call x1, Pallas kernels, on_device(): pl.pallas_call(kernel, out_shape=(out, out, out, pltpu.VMEM((LV_ALL, n),...  51.8 us
    unnamed x4, local copies, waits for them, and re-layouts  3.51 us

profile of v3, /device:TPU:1, one launch (start us, length us, event | category | flops | bytes accessed | tf_op | source)
XLA Modules:
  0.0 56.0 jit_solution(12078229472337683500)
XLA Ops:
  0.6 51.8 %shard_map.102 = (f32[256,1024]{1,0:T(8,128)S(1)}, f32[256,1024]{1,0:T(8,128)S(1)}, f32[256,1024]{1,0:T(8,128)S(1)}, f32[7,256]{1,0:T(8,128)S(1)}) custom-call(f32[8,256]{1,0:T(8,128)} %bitcast.5, f32[7,256]{1,0:T(8,128)} %bitcast.6, s32[1,256]{1,0:T(1,128)} %bitcast.7, f32[256,1024]{1,0:T(8,128)} %q_hbm.1, f32[256,1024]{1,0:T(8,128)} %k_hbm.1, ...), custom_call_target="tpu_custom_call" | custom-call | tf_op jit(solution)/shard_map/pallas_call | solution.py:849
  52.5 1.0 %copy.15 = f32[256,1024]{1,0:T(8,128)} copy(f32[256,1024]{1,0:T(8,128)S(1)} %get-tuple-element.12) | data formatting | bytes 2097152
  53.4 0.6 %copy.18 = f32[256,7]{0,1:T(8,128)} copy(f32[256,7]{0,1:T(8,128)S(1)} %bitcast.4) | data formatting | bytes 14336
  54.0 1.0 %copy.16 = f32[256,1024]{1,0:T(8,128)} copy(f32[256,1024]{1,0:T(8,128)S(1)} %get-tuple-element.13) | data formatting | bytes 2097152
  55.0 1.0 %copy.17 = f32[256,1024]{1,0:T(8,128)} copy(f32[256,1024]{1,0:T(8,128)S(1)} %get-tuple-element.14) | data formatting | bytes 2097152
